TPU v7x, 256 devices: a whole 4x4x8 slice. The times are simulated.
256 devices in a mesh: scan: 64 (over x, y_hi, z), tile: 4 (over y_lo, core).
Axes of the slice: x: 4, y: 4 (y_hi: 2, y_lo: 2; y = y_hi * 2 + y_lo), z: 8, core: 2. Of those that a mesh axis runs over, the one named last changes fastest.
Arguments:
- probe_modes: float32 [3072, 256], P(('scan', 'tile')), may hold values from -2.1 to 2.1
- object_tiles: float32 [4, 2, 2, 320, 320], P('tile'), may hold values from -4 to 4
- scan_offsets: int32 [512, 2], P(('scan', 'tile')), may hold values from 0 to 64, as said below
- patch_tiles: int32 [512], P(('scan', 'tile')), may hold values from 0 to 3, as said below
- amplitudes: bfloat16 [512, 256, 256], P(('scan', 'tile')), may hold values from 0.5 to 20
Outputs:
- probe_gradient: float32 [3072, 256], P(('scan', 'tile'))
- object_gradient: float32 [4, 2, 2, 320, 320], P('tile', None, None, 'scan')
Inputs may be any that keep to these rules, and one draw needn't show every extreme that they name: `patch_tiles`: each entry names the tile that wholly holds the patch of its position. `scan_offsets`: every patch lies wholly inside its tile.
All inputs are finite; a program needn't handle non-finite values.
Results may differ from a plain program's by a relative error of at most 0.02.
Values sent between devices are 32-bit elements; how exact they have to be, the bound alone decides.
No kernel may reach another device: no remote copies, remote signals or barrier semaphores. Data moves between devices by JAX's collectives and lax.ppermute only.
A program may use at most 128 MiB of HBM per device.

v0:
```python
import math

import jax
import jax.numpy as jnp
from jax import lax
from jax.sharding import PartitionSpec as P


def complex_tables(pixels):
    pixel_index = jnp.arange(pixels, dtype=jnp.int32)
    offset = pixel_index[:, None] - pixel_index[None, :]
    chirp_phase = (offset * offset % (2 * pixels)).astype(jnp.float32) * (math.pi / pixels)
    product = (pixel_index[:, None] * pixel_index[None, :] % pixels).astype(jnp.float32) * (
        2.0 * math.pi / pixels
    )
    norm_scale = 1.0 / math.sqrt(pixels)
    fresnel = (jnp.stack([jnp.cos(chirp_phase), jnp.sin(chirp_phase)]) * norm_scale).astype(
        jnp.bfloat16
    )
    spectral = (jnp.stack([jnp.cos(product), -jnp.sin(product)]) * norm_scale).astype(jnp.bfloat16)
    return (fresnel, spectral)


def multiply_object(exit_wave, object_patch):
    real_part = exit_wave[0] * object_patch[0] - exit_wave[1] * object_patch[1]
    imag_part = exit_wave[0] * object_patch[1] + exit_wave[1] * object_patch[0]
    return jnp.stack([real_part, imag_part])


def left_side(matrix_part, component):
    return jnp.einsum("ij,mjk->mik", matrix_part, component, preferred_element_type=jnp.float32)


def right_side(component, matrix_part):
    return jnp.einsum("mik,jk->mij", component, matrix_part, preferred_element_type=jnp.float32)


def left_product(matrix, exit_wave):
    real_part = left_side(matrix[0], exit_wave[0]) - left_side(matrix[1], exit_wave[1])
    imag_part = left_side(matrix[0], exit_wave[1]) + left_side(matrix[1], exit_wave[0])
    return jnp.stack([real_part, imag_part])


def right_product(exit_wave, matrix):
    real_part = right_side(exit_wave[0], matrix[0]) - right_side(exit_wave[1], matrix[1])
    imag_part = right_side(exit_wave[0], matrix[1]) + right_side(exit_wave[1], matrix[0])
    return jnp.stack([real_part, imag_part])


def position_loss(probe_values, patch_values, amplitude, fresnel, spectral):
    exit_wave = probe_values
    layers = patch_values.shape[0]
    for slice_index in range(layers):
        exit_wave = multiply_object(exit_wave, patch_values[slice_index])
        matrix = fresnel if slice_index < layers - 1 else spectral
        rounded = exit_wave.astype(jnp.bfloat16)
        halfway = left_product(matrix, rounded).astype(jnp.bfloat16)
        exit_wave = right_product(halfway, matrix)
    intensity = jnp.sum(exit_wave * exit_wave, axis=(0, 1))
    residue = jnp.sqrt(intensity + 1.0) - amplitude.astype(jnp.float32)
    return jnp.sum(residue * residue)


def body(probe_modes, object_tiles, scan_offsets, patch_tiles, amplitudes):
    tile_count = lax.axis_size("tile")
    scan_count = lax.axis_size("scan")
    pixels = probe_modes.shape[1]
    layers = object_tiles.shape[1]
    side = object_tiles.shape[3]
    whole_probe = lax.all_gather(probe_modes, ("scan", "tile"), axis=0, tiled=True)
    probe_field = whole_probe.reshape(2, -1, pixels, pixels)
    fresnel, spectral = complex_tables(pixels)
    whole_object = lax.all_gather(object_tiles, "tile", axis=0, tiled=True)

    def cut_own(tile_number, corner):
        anchor = (tile_number, jnp.int32(0), jnp.int32(0), corner[0], corner[1])
        return lax.dynamic_slice(whole_object, anchor, (1, layers, 2, pixels, pixels))[0]

    own_patches = jax.vmap(cut_own)(patch_tiles, scan_offsets)

    def one_position(probe_total, inputs):
        object_patch, amplitude = inputs

        def local_loss(probe_values, patch_values):
            return position_loss(probe_values, patch_values, amplitude, fresnel, spectral)

        misfit, pullback = jax.vjp(local_loss, probe_field, object_patch)
        probe_part, patch_part = pullback(jnp.ones_like(misfit))
        return (probe_total + probe_part, patch_part)

    probe_total, patch_gradients = lax.scan(
        one_position, jnp.zeros_like(probe_field), (own_patches, amplitudes)
    )

    def add_patch(object_total, inputs):
        gradient_piece, tile_number, corner = inputs
        anchor = (tile_number, jnp.int32(0), jnp.int32(0), corner[0], corner[1])
        current = lax.dynamic_slice(object_total, anchor, (1,) + gradient_piece.shape)
        return (
            lax.dynamic_update_slice(object_total, current + gradient_piece[None], anchor),
            None,
        )

    whole_shape = (tile_count,) + object_tiles.shape[1:]
    object_total, _ = lax.scan(
        add_patch, jnp.zeros(whole_shape, jnp.float32), (patch_gradients, patch_tiles, scan_offsets)
    )
    row_count = side // scan_count
    arranged = object_total.reshape(tile_count, layers, 2, scan_count, row_count, side)
    arranged = arranged.transpose(3, 0, 1, 2, 4, 5).reshape(
        scan_count * tile_count, layers, 2, row_count, side
    )
    object_gradient = lax.psum_scatter(arranged, ("scan", "tile"), scatter_dimension=0, tiled=True)
    probe_gradient = lax.psum_scatter(
        probe_total.reshape(-1, pixels), ("scan", "tile"), scatter_dimension=0, tiled=True
    )
    return (probe_gradient, object_gradient)


def solution(mesh):
    placed = (
        P(("scan", "tile"), None),
        P("tile", None, None, None, None),
        P(("scan", "tile"), None),
        P(("scan", "tile")),
        P(("scan", "tile"), None, None),
    )
    return jax.shard_map(
        body,
        mesh=mesh,
        in_specs=placed,
        out_specs=(P(("scan", "tile"), None), P("tile", None, None, "scan", None)),
        check_vma=False,
    )
```

profile of v0, /device:TPU:6, one launch (start us, length us, event | category | flops | bytes accessed | tf_op | source)
XLA Modules:
  0.0 2016.1 jit_solution(5033408186173666694)
XLA Ops:
  12.0 415.8 %all-gather.6.cloned.1.call-done = f32[256,12,256]{2,1,0:T(8,128)} async-done(((f32[1,12,256]{2,1,0:T(8,128)}), f32[256,12,256]{2,1,0:T(8,128)}) %all-gather.6.cloned.1.call-update) | async-done | bytes 3145744 | tf_op jit(solution)/shard_map/all_gather | solution.py:70
  434.8 72.6 %all-gather.4.cloned.1.call-done = f32[4,2,2,320,320]{4,3,2,1,0:T(8,128)} async-done(((f32[1,2,2,320,320]{4,3,2,1,0:T(8,128)}), f32[4,2,2,320,320]{4,3,2,1,0:T(8,128)}) %all-gather.4.cloned.1.call-update) | async-done | bytes 6553616 | tf_op jit(solution)/shard_map/all_gather | solution.py:73
  507.3 10.7 while.25
  518.1 110.2 %while.26 = (s32[]{:T(128)}, f32[2,6,256,256]{2,3,1,0:T(8,128)}, f32[2,2,2,256,256]{4,3,2,1,0:T(8,128)}, f32[2,6,256,256]{2,3,1,0:T(8,128)S(1)}, f32[2,2,2,256,2...) while((s32[]{:T(128)}, f32[2,6,256,256]{2,3,1,0:T(8,128)}, ...), condition=%wide.region_10.11_spmd.clone, body=%wide.region_0.10_spmd.clone.sunk | while | flops 6493634560 | bytes 218235760 | solution.py:91
  573.4 5.2 select_add_fusion.2
  622.1 6.1 select_add_fusion.2
  628.3 5.7 broadcast_in_dim.99.clone
  634.0 202.0 %while.24 = (s32[]{:T(128)}, f32[4,2,2,320,320]{4,2,3,1,0:T(2,128)}, s32[2]{0:T(128)S(1)}, s32[2,2]{1,0:T(2,128)S(1)}, f32[2,2,2,256,256]{4,3,2,1,0:T(8,128)}, /*index=5*/s32[]{:T(128)}, s32[]{:T(128)}, s32[]{:T(128)}, s32[]{:T(128)}) while((s32[]{:T(128)}, f32[4,2,2,320,320]{4,2,3,1,0:T(2,128)}, s32[2]{0:T(128)S(1)}, ...), condition=%wide.region_13.14_spmd, body=%wide.region_12.13_spmd.sunk | while | flops 262155 | bytes 9437447 | solution.py:105
  645.7 89.2 %dynamic_update_slice.11 = f32[4,2,2,320,320]{4,2,3,1,0:T(2,128)} dynamic-update-slice(f32[4,2,2,320,320]{4,2,3,1,0:T(2,128)} %get-tuple-element.452, f32[1,2,2,256,256]{4,2,3,1,0:T(2,128)S(1)} %copy.201, s32[]{:T(128)S(6)} %select_n.91, s32[]{:T(128)} %constant.64.clone.1..sunk, s32[]{:T(128)} %constant.64.clone.1..sunk, s32[]{:T(128)S(6)} %select_n.92, s32[]{:T(128)S(6)} %select_n.93) | dynamic-update-slice | bytes 2097156 | tf_op jit(solution)/shard_map/while/body/eval_jaxpr/dynamic_update_slice | solution.py:100
  746.7 89.2 %dynamic_update_slice.11 = f32[4,2,2,320,320]{4,2,3,1,0:T(2,128)} dynamic-update-slice(f32[4,2,2,320,320]{4,2,3,1,0:T(2,128)} %get-tuple-element.452, f32[1,2,2,256,256]{4,2,3,1,0:T(2,128)S(1)} %copy.201, s32[]{:T(128)S(6)} %select_n.91, s32[]{:T(128)} %constant.64.clone.1..sunk, s32[]{:T(128)} %constant.64.clone.1..sunk, s32[]{:T(128)S(6)} %select_n.92, s32[]{:T(128)S(6)} %select_n.93) | dynamic-update-slice | bytes 2097156 | tf_op jit(solution)/shard_map/while/body/eval_jaxpr/dynamic_update_slice | solution.py:100
  836.0 9.0 copy.163
  849.2 592.6 %fusion = f32[16,256]{1,0:T(8,128)S(1)} fusion(f32[3072,256]{1,0:T(8,128)} %bitcast.555), kind=kCustom, calls=%all-reduce-scatter | all-reduce-scatter fusion | flops 1048577 | bytes 3162112
  1441.8 79.9 %collective-permute-start = (f32[16,256]{1,0:T(8,128)S(1)}, f32[16,256]{1,0:T(8,128)S(1)}, u32[]{:S(2)}, u32[]{:S(2)}) collective-permute-start(f32[16,256]{1,0:T(8,128)S(1)} %fusion), channel_id=1, source_target_pairs={{0,1},{1,2},{2,3},{3,4},{4,5},{5,6},{6,7},{7,8},{8,9},{9,10},{10,1... | collective-permute-start | bytes 49160
  1521.7 13.2 collective-permute-start.1
  1535.0 13.1 collective-permute-start.10
  1549.4 14.9 collective-permute-start.11
  1564.4 13.1 collective-permute-start.12
  1577.5 13.1 collective-permute-start.13
  1590.6 13.1 collective-permute-start.14
  1603.8 13.1 collective-permute-start.15
  1616.9 13.1 collective-permute-start.16
  1630.1 13.1 collective-permute-start.17
  1643.2 13.1 collective-permute-start.18
  1656.3 13.1 collective-permute-start.19
  1669.5 13.1 collective-permute-start.2
  1682.6 13.1 collective-permute-start.20
  1695.8 13.1 collective-permute-start.21
  1708.9 13.1 collective-permute-start.22
  1722.0 13.1 collective-permute-start.23
  1735.2 13.1 collective-permute-start.24
  1748.3 13.1 collective-permute-start.25
  1761.5 13.1 collective-permute-start.26
  1774.6 13.1 collective-permute-start.27
  1787.7 6.1 collective-permute-start.28
  1793.9 5.0 collective-permute-start.29
  1798.9 8.7 collective-permute-start.3
  1807.7 7.1 collective-permute-start.30
  1834.3 17.7 collective-permute-start.4
  1852.0 7.0 collective-permute-start.40
  1879.8 20.8 %collective-permute-start.5 = (f32[16,256]{1,0:T(8,128)S(1)}, f32[16,256]{1,0:T(8,128)S(1)}, u32[]{:S(2)}, u32[]{:S(2)}) collective-permute-start(f32[16,256]{1,0:T(8,128)S(1)} %fusion), channel_id=1, source_target_pairs={{0,6},{1,7},{2,8},{3,9},{4,10},{5,11},{6,12},{7,13},{8,14},{9,15},... | collective-permute-start | bytes 49160
  1900.6 10.3 collective-permute-start.50
  1928.6 13.3 collective-permute-start.6
  1941.9 8.0 collective-permute-start.60
  1953.7 9.8 collective-permute-start.7
  1963.5 13.1 collective-permute-start.8
  1976.6 13.1 collective-permute-start.9
  1989.8 10.1 collective-permute-done.9
  1999.9 7.2 concatenate.5
  (287 shorter events, 189.6 us)
Async XLA Ops:
  7.2 420.6 %all-gather.6.cloned.1.call-start = ((), (), s32[]{:S(2)}) async-start(), calls=%async_computation.1 | async-start | bytes 4210688 | tf_op jit(solution)/shard_map/all_gather | solution.py:70
  7.9 499.4 %all-gather.4.cloned.1.call-start = ((), (), s32[]{:S(2)}) async-start(), calls=%async_computation | async-start | bytes 9830400 | tf_op jit(solution)/shard_map/all_gather | solution.py:73
  8.7 1999.1 %all-reduce.39.cloned.1.call-start = ((), (), s32[]{:S(2)}) async-start(), calls=%async_computation.2 | async-start | bytes 15728640
  1441.8 135.7 %collective-permute-start = (f32[16,256]{1,0:T(8,128)S(1)}, f32[16,256]{1,0:T(8,128)S(1)}, u32[]{:S(2)}, u32[]{:S(2)}) collective-permute-start(f32[16,256]{1,0:T(8,128)S(1)} %fusion), channel_id=1, source_target_pairs={{0,1},{1,2},{2,3},{3,4},{4,5},{5,6},{6,7},{7,8},{8,9},{9,10},{10,1... | collective-permute-start | bytes 49160
  1521.7 68.9 %collective-permute-start.1 = (f32[16,256]{1,0:T(8,128)S(1)}, f32[16,256]{1,0:T(8,128)S(1)}, u32[]{:S(2)}, u32[]{:S(2)}) collective-permute-start(f32[16,256]{1,0:T(8,128)S(1)} %fusion), channel_id=1, source_target_pairs={{0,2},{1,3},{2,4},{3,5},{4,6},{5,7},{6,8},{7,9},{8,10},{9,11},{10,... | collective-permute-start | bytes 49160
  1535.0 68.8 %collective-permute-start.10 = (f32[16,256]{1,0:T(8,128)S(1)}, f32[16,256]{1,0:T(8,128)S(1)}, u32[]{:S(2)}, u32[]{:S(2)}) collective-permute-start(f32[16,256]{1,0:T(8,128)S(1)} %fusion), channel_id=1, source_target_pairs={{0,11},{1,12},{2,13},{3,14},{4,15},{5,16},{6,17},{7,18},{8,19},{9,... | collective-permute-start | bytes 49160
  1549.4 67.5 %collective-permute-start.11 = (f32[16,256]{1,0:T(8,128)S(1)}, f32[16,256]{1,0:T(8,128)S(1)}, u32[]{:S(2)}, u32[]{:S(2)}) collective-permute-start(f32[16,256]{1,0:T(8,128)S(1)} %fusion), channel_id=1, source_target_pairs={{0,12},{1,13},{2,14},{3,15},{4,16},{5,17},{6,18},{7,19},{8,20},{9,... | collective-permute-start | bytes 49160
  1564.4 65.7 %collective-permute-start.12 = (f32[16,256]{1,0:T(8,128)S(1)}, f32[16,256]{1,0:T(8,128)S(1)}, u32[]{:S(2)}, u32[]{:S(2)}) collective-permute-start(f32[16,256]{1,0:T(8,128)S(1)} %fusion), channel_id=1, source_target_pairs={{0,13},{1,14},{2,15},{3,16},{4,17},{5,18},{6,19},{7,20},{8,21},{9,... | collective-permute-start | bytes 49160
  1577.5 65.7 %collective-permute-start.13 = (f32[16,256]{1,0:T(8,128)S(1)}, f32[16,256]{1,0:T(8,128)S(1)}, u32[]{:S(2)}, u32[]{:S(2)}) collective-permute-start(f32[16,256]{1,0:T(8,128)S(1)} %fusion), channel_id=1, source_target_pairs={{0,14},{1,15},{2,16},{3,17},{4,18},{5,19},{6,20},{7,21},{8,22},{9,... | collective-permute-start | bytes 49160
  1590.6 65.7 %collective-permute-start.14 = (f32[16,256]{1,0:T(8,128)S(1)}, f32[16,256]{1,0:T(8,128)S(1)}, u32[]{:S(2)}, u32[]{:S(2)}) collective-permute-start(f32[16,256]{1,0:T(8,128)S(1)} %fusion), channel_id=1, source_target_pairs={{0,15},{1,16},{2,17},{3,18},{4,19},{5,20},{6,21},{7,22},{8,23},{9,... | collective-permute-start | bytes 49160
  1603.8 65.7 %collective-permute-start.15 = (f32[16,256]{1,0:T(8,128)S(1)}, f32[16,256]{1,0:T(8,128)S(1)}, u32[]{:S(2)}, u32[]{:S(2)}) collective-permute-start(f32[16,256]{1,0:T(8,128)S(1)} %fusion), channel_id=1, source_target_pairs={{0,16},{1,17},{2,18},{3,19},{4,20},{5,21},{6,22},{7,23},{8,24},{9,... | collective-permute-start | bytes 49160
  1616.9 65.7 %collective-permute-start.16 = (f32[16,256]{1,0:T(8,128)S(1)}, f32[16,256]{1,0:T(8,128)S(1)}, u32[]{:S(2)}, u32[]{:S(2)}) collective-permute-start(f32[16,256]{1,0:T(8,128)S(1)} %fusion), channel_id=1, source_target_pairs={{0,17},{1,18},{2,19},{3,20},{4,21},{5,22},{6,23},{7,24},{8,25},{9,... | collective-permute-start | bytes 49160
  1630.1 65.7 %collective-permute-start.17 = (f32[16,256]{1,0:T(8,128)S(1)}, f32[16,256]{1,0:T(8,128)S(1)}, u32[]{:S(2)}, u32[]{:S(2)}) collective-permute-start(f32[16,256]{1,0:T(8,128)S(1)} %fusion), channel_id=1, source_target_pairs={{0,18},{1,19},{2,20},{3,21},{4,22},{5,23},{6,24},{7,25},{8,26},{9,... | collective-permute-start | bytes 49160
  1643.2 65.7 %collective-permute-start.18 = (f32[16,256]{1,0:T(8,128)S(1)}, f32[16,256]{1,0:T(8,128)S(1)}, u32[]{:S(2)}, u32[]{:S(2)}) collective-permute-start(f32[16,256]{1,0:T(8,128)S(1)} %fusion), channel_id=1, source_target_pairs={{0,19},{1,20},{2,21},{3,22},{4,23},{5,24},{6,25},{7,26},{8,27},{9,... | collective-permute-start | bytes 49160
  1656.3 65.7 %collective-permute-start.19 = (f32[16,256]{1,0:T(8,128)S(1)}, f32[16,256]{1,0:T(8,128)S(1)}, u32[]{:S(2)}, u32[]{:S(2)}) collective-permute-start(f32[16,256]{1,0:T(8,128)S(1)} %fusion), channel_id=1, source_target_pairs={{0,20},{1,21},{2,22},{3,23},{4,24},{5,25},{6,26},{7,27},{8,28},{9,... | collective-permute-start | bytes 49160
  1669.5 65.7 %collective-permute-start.2 = (f32[16,256]{1,0:T(8,128)S(1)}, f32[16,256]{1,0:T(8,128)S(1)}, u32[]{:S(2)}, u32[]{:S(2)}) collective-permute-start(f32[16,256]{1,0:T(8,128)S(1)} %fusion), channel_id=1, source_target_pairs={{0,3},{1,4},{2,5},{3,6},{4,7},{5,8},{6,9},{7,10},{8,11},{9,12},{10... | collective-permute-start | bytes 49160
  1682.6 65.7 %collective-permute-start.20 = (f32[16,256]{1,0:T(8,128)S(1)}, f32[16,256]{1,0:T(8,128)S(1)}, u32[]{:S(2)}, u32[]{:S(2)}) collective-permute-start(f32[16,256]{1,0:T(8,128)S(1)} %fusion), channel_id=1, source_target_pairs={{0,21},{1,22},{2,23},{3,24},{4,25},{5,26},{6,27},{7,28},{8,29},{9,... | collective-permute-start | bytes 49160
  1695.8 65.7 %collective-permute-start.21 = (f32[16,256]{1,0:T(8,128)S(1)}, f32[16,256]{1,0:T(8,128)S(1)}, u32[]{:S(2)}, u32[]{:S(2)}) collective-permute-start(f32[16,256]{1,0:T(8,128)S(1)} %fusion), channel_id=1, source_target_pairs={{0,22},{1,23},{2,24},{3,25},{4,26},{5,27},{6,28},{7,29},{8,30},{9,... | collective-permute-start | bytes 49160
  1708.9 65.7 %collective-permute-start.22 = (f32[16,256]{1,0:T(8,128)S(1)}, f32[16,256]{1,0:T(8,128)S(1)}, u32[]{:S(2)}, u32[]{:S(2)}) collective-permute-start(f32[16,256]{1,0:T(8,128)S(1)} %fusion), channel_id=1, source_target_pairs={{0,23},{1,24},{2,25},{3,26},{4,27},{5,28},{6,29},{7,30},{8,31},{9,... | collective-permute-start | bytes 49160
  1722.0 65.7 %collective-permute-start.23 = (f32[16,256]{1,0:T(8,128)S(1)}, f32[16,256]{1,0:T(8,128)S(1)}, u32[]{:S(2)}, u32[]{:S(2)}) collective-permute-start(f32[16,256]{1,0:T(8,128)S(1)} %fusion), channel_id=1, source_target_pairs={{0,24},{1,25},{2,26},{3,27},{4,28},{5,29},{6,30},{7,31},{8,32},{9,... | collective-permute-start | bytes 49160
  1735.2 58.7 %collective-permute-start.24 = (f32[16,256]{1,0:T(8,128)S(1)}, f32[16,256]{1,0:T(8,128)S(1)}, u32[]{:S(2)}, u32[]{:S(2)}) collective-permute-start(f32[16,256]{1,0:T(8,128)S(1)} %fusion), channel_id=1, source_target_pairs={{0,25},{1,26},{2,27},{3,28},{4,29},{5,30},{6,31},{7,32},{8,33},{9,... | collective-permute-start | bytes 49160
  1748.3 50.6 %collective-permute-start.25 = (f32[16,256]{1,0:T(8,128)S(1)}, f32[16,256]{1,0:T(8,128)S(1)}, u32[]{:S(2)}, u32[]{:S(2)}) collective-permute-start(f32[16,256]{1,0:T(8,128)S(1)} %fusion), channel_id=1, source_target_pairs={{0,26},{1,27},{2,28},{3,29},{4,30},{5,31},{6,32},{7,33},{8,34},{9,... | collective-permute-start | bytes 49160
  1761.5 46.2 %collective-permute-start.26 = (f32[16,256]{1,0:T(8,128)S(1)}, f32[16,256]{1,0:T(8,128)S(1)}, u32[]{:S(2)}, u32[]{:S(2)}) collective-permute-start(f32[16,256]{1,0:T(8,128)S(1)} %fusion), channel_id=1, source_target_pairs={{0,27},{1,28},{2,29},{3,30},{4,31},{5,32},{6,33},{7,34},{8,35},{9,... | collective-permute-start | bytes 49160
  1774.6 40.1 %collective-permute-start.27 = (f32[16,256]{1,0:T(8,128)S(1)}, f32[16,256]{1,0:T(8,128)S(1)}, u32[]{:S(2)}, u32[]{:S(2)}) collective-permute-start(f32[16,256]{1,0:T(8,128)S(1)} %fusion), channel_id=1, source_target_pairs={{0,28},{1,29},{2,30},{3,31},{4,32},{5,33},{6,34},{7,35},{8,36},{9,... | collective-permute-start | bytes 49160
  1787.7 31.1 %collective-permute-start.28 = (f32[16,256]{1,0:T(8,128)S(1)}, f32[16,256]{1,0:T(8,128)S(1)}, u32[]{:S(2)}, u32[]{:S(2)}) collective-permute-start(f32[16,256]{1,0:T(8,128)S(1)} %fusion), channel_id=1, source_target_pairs={{0,29},{1,30},{2,31},{3,32},{4,33},{5,34},{6,35},{7,36},{8,37},{9,... | collective-permute-start | bytes 49160
  1793.9 26.9 %collective-permute-start.29 = (f32[16,256]{1,0:T(8,128)S(1)}, f32[16,256]{1,0:T(8,128)S(1)}, u32[]{:S(2)}, u32[]{:S(2)}) collective-permute-start(f32[16,256]{1,0:T(8,128)S(1)} %fusion), channel_id=1, source_target_pairs={{0,30},{1,31},{2,32},{3,33},{4,34},{5,35},{6,36},{7,37},{8,38},{9,... | collective-permute-start | bytes 49160
  1798.9 23.8 %collective-permute-start.3 = (f32[16,256]{1,0:T(8,128)S(1)}, f32[16,256]{1,0:T(8,128)S(1)}, u32[]{:S(2)}, u32[]{:S(2)}) collective-permute-start(f32[16,256]{1,0:T(8,128)S(1)} %fusion), channel_id=1, source_target_pairs={{0,4},{1,5},{2,6},{3,7},{4,8},{5,9},{6,10},{7,11},{8,12},{9,13},{1... | collective-permute-start | bytes 49160
  1826.6 25.4 %collective-permute-start.36 = (f32[16,256]{1,0:T(8,128)S(1)}, f32[16,256]{1,0:T(8,128)S(1)}, u32[]{:S(2)}, u32[]{:S(2)}) collective-permute-start(f32[16,256]{1,0:T(8,128)S(1)} %fusion), channel_id=1, source_target_pairs={{0,37},{1,38},{2,39},{3,40},{4,41},{5,42},{6,43},{7,44},{8,45},{9,... | collective-permute-start | bytes 49160
  1828.5 30.5 %collective-permute-start.37 = (f32[16,256]{1,0:T(8,128)S(1)}, f32[16,256]{1,0:T(8,128)S(1)}, u32[]{:S(2)}, u32[]{:S(2)}) collective-permute-start(f32[16,256]{1,0:T(8,128)S(1)} %fusion), channel_id=1, source_target_pairs={{0,38},{1,39},{2,40},{3,41},{4,42},{5,43},{6,44},{7,45},{8,46},{9,... | collective-permute-start | bytes 49160
  1830.4 30.5 %collective-permute-start.38 = (f32[16,256]{1,0:T(8,128)S(1)}, f32[16,256]{1,0:T(8,128)S(1)}, u32[]{:S(2)}, u32[]{:S(2)}) collective-permute-start(f32[16,256]{1,0:T(8,128)S(1)} %fusion), channel_id=1, source_target_pairs={{0,39},{1,40},{2,41},{3,42},{4,43},{5,44},{6,45},{7,46},{8,47},{9,... | collective-permute-start | bytes 49160
  1832.4 30.5 %collective-permute-start.39 = (f32[16,256]{1,0:T(8,128)S(1)}, f32[16,256]{1,0:T(8,128)S(1)}, u32[]{:S(2)}, u32[]{:S(2)}) collective-permute-start(f32[16,256]{1,0:T(8,128)S(1)} %fusion), channel_id=1, source_target_pairs={{0,40},{1,41},{2,42},{3,43},{4,44},{5,45},{6,46},{7,47},{8,48},{9,... | collective-permute-start | bytes 49160
  1834.3 30.5 %collective-permute-start.4 = (f32[16,256]{1,0:T(8,128)S(1)}, f32[16,256]{1,0:T(8,128)S(1)}, u32[]{:S(2)}, u32[]{:S(2)}) collective-permute-start(f32[16,256]{1,0:T(8,128)S(1)} %fusion), channel_id=1, source_target_pairs={{0,5},{1,6},{2,7},{3,8},{4,9},{5,10},{6,11},{7,12},{8,13},{9,14},{... | collective-permute-start | bytes 49160
  1869.7 30.9 %collective-permute-start.46 = (f32[16,256]{1,0:T(8,128)S(1)}, f32[16,256]{1,0:T(8,128)S(1)}, u32[]{:S(2)}, u32[]{:S(2)}) collective-permute-start(f32[16,256]{1,0:T(8,128)S(1)} %fusion), channel_id=1, source_target_pairs={{0,47},{1,48},{2,49},{3,50},{4,51},{5,52},{6,53},{7,54},{8,55},{9,... | collective-permute-start | bytes 49160
  1871.6 39.3 %collective-permute-start.47 = (f32[16,256]{1,0:T(8,128)S(1)}, f32[16,256]{1,0:T(8,128)S(1)}, u32[]{:S(2)}, u32[]{:S(2)}) collective-permute-start(f32[16,256]{1,0:T(8,128)S(1)} %fusion), channel_id=1, source_target_pairs={{0,48},{1,49},{2,50},{3,51},{4,52},{5,53},{6,54},{7,55},{8,56},{9,... | collective-permute-start | bytes 49160
  1875.9 36.9 %collective-permute-start.48 = (f32[16,256]{1,0:T(8,128)S(1)}, f32[16,256]{1,0:T(8,128)S(1)}, u32[]{:S(2)}, u32[]{:S(2)}) collective-permute-start(f32[16,256]{1,0:T(8,128)S(1)} %fusion), channel_id=1, source_target_pairs={{0,49},{1,50},{2,51},{3,52},{4,53},{5,54},{6,55},{7,56},{8,57},{9,... | collective-permute-start | bytes 49160
  1877.8 36.9 %collective-permute-start.49 = (f32[16,256]{1,0:T(8,128)S(1)}, f32[16,256]{1,0:T(8,128)S(1)}, u32[]{:S(2)}, u32[]{:S(2)}) collective-permute-start(f32[16,256]{1,0:T(8,128)S(1)} %fusion), channel_id=1, source_target_pairs={{0,50},{1,51},{2,52},{3,53},{4,54},{5,55},{6,56},{7,57},{8,58},{9,... | collective-permute-start | bytes 49160
  1879.8 37.1 %collective-permute-start.5 = (f32[16,256]{1,0:T(8,128)S(1)}, f32[16,256]{1,0:T(8,128)S(1)}, u32[]{:S(2)}, u32[]{:S(2)}) collective-permute-start(f32[16,256]{1,0:T(8,128)S(1)} %fusion), channel_id=1, source_target_pairs={{0,6},{1,7},{2,8},{3,9},{4,10},{5,11},{6,12},{7,13},{8,14},{9,15},... | collective-permute-start | bytes 49160
  1920.8 21.0 %collective-permute-start.56 = (f32[16,256]{1,0:T(8,128)S(1)}, f32[16,256]{1,0:T(8,128)S(1)}, u32[]{:S(2)}, u32[]{:S(2)}) collective-permute-start(f32[16,256]{1,0:T(8,128)S(1)} %fusion), channel_id=1, source_target_pairs={{0,57},{1,58},{2,59},{3,60},{4,61},{5,62},{6,63},{7,64},{8,65},{9,... | collective-permute-start | bytes 49160
  1922.8 27.1 %collective-permute-start.57 = (f32[16,256]{1,0:T(8,128)S(1)}, f32[16,256]{1,0:T(8,128)S(1)}, u32[]{:S(2)}, u32[]{:S(2)}) collective-permute-start(f32[16,256]{1,0:T(8,128)S(1)} %fusion), channel_id=1, source_target_pairs={{0,58},{1,59},{2,60},{3,61},{4,62},{5,63},{6,64},{7,65},{8,66},{9,... | collective-permute-start | bytes 49160
  1924.7 27.1 %collective-permute-start.58 = (f32[16,256]{1,0:T(8,128)S(1)}, f32[16,256]{1,0:T(8,128)S(1)}, u32[]{:S(2)}, u32[]{:S(2)}) collective-permute-start(f32[16,256]{1,0:T(8,128)S(1)} %fusion), channel_id=1, source_target_pairs={{0,59},{1,60},{2,61},{3,62},{4,63},{5,64},{6,65},{7,66},{8,67},{9,... | collective-permute-start | bytes 49160
  1926.6 27.1 %collective-permute-start.59 = (f32[16,256]{1,0:T(8,128)S(1)}, f32[16,256]{1,0:T(8,128)S(1)}, u32[]{:S(2)}, u32[]{:S(2)}) collective-permute-start(f32[16,256]{1,0:T(8,128)S(1)} %fusion), channel_id=1, source_target_pairs={{0,60},{1,61},{2,62},{3,63},{4,64},{5,65},{6,66},{7,67},{8,68},{9,... | collective-permute-start | bytes 49160
  1928.6 34.9 %collective-permute-start.6 = (f32[16,256]{1,0:T(8,128)S(1)}, f32[16,256]{1,0:T(8,128)S(1)}, u32[]{:S(2)}, u32[]{:S(2)}) collective-permute-start(f32[16,256]{1,0:T(8,128)S(1)} %fusion), channel_id=1, source_target_pairs={{0,7},{1,8},{2,9},{3,10},{4,11},{5,12},{6,13},{7,14},{8,15},{9,16}... | collective-permute-start | bytes 49160
  1941.9 34.8 %collective-permute-start.60 = (f32[16,256]{1,0:T(8,128)S(1)}, f32[16,256]{1,0:T(8,128)S(1)}, u32[]{:S(2)}, u32[]{:S(2)}) collective-permute-start(f32[16,256]{1,0:T(8,128)S(1)} %fusion), channel_id=1, source_target_pairs={{0,61},{1,62},{2,63},{3,64},{4,65},{5,66},{6,67},{7,68},{8,69},{9,... | collective-permute-start | bytes 49160
  1949.9 39.9 %collective-permute-start.61 = (f32[16,256]{1,0:T(8,128)S(1)}, f32[16,256]{1,0:T(8,128)S(1)}, u32[]{:S(2)}, u32[]{:S(2)}) collective-permute-start(f32[16,256]{1,0:T(8,128)S(1)} %fusion), channel_id=1, source_target_pairs={{0,62},{1,63},{2,64},{3,65},{4,66},{5,67},{6,68},{7,69},{8,70},{9,... | collective-permute-start | bytes 49160
  1951.8 38.0 %collective-permute-start.62 = (f32[16,256]{1,0:T(8,128)S(1)}, f32[16,256]{1,0:T(8,128)S(1)}, u32[]{:S(2)}, u32[]{:S(2)}) collective-permute-start(f32[16,256]{1,0:T(8,128)S(1)} %fusion), channel_id=1, source_target_pairs={{0,63},{1,64},{2,65},{3,66},{4,67},{5,68},{6,69},{7,70},{8,71},{9,... | collective-permute-start | bytes 49160
  1953.7 36.1 %collective-permute-start.7 = (f32[16,256]{1,0:T(8,128)S(1)}, f32[16,256]{1,0:T(8,128)S(1)}, u32[]{:S(2)}, u32[]{:S(2)}) collective-permute-start(f32[16,256]{1,0:T(8,128)S(1)} %fusion), channel_id=1, source_target_pairs={{0,8},{1,9},{2,10},{3,11},{4,12},{5,13},{6,14},{7,15},{8,16},{9,17... | collective-permute-start | bytes 49160
  1963.5 26.3 %collective-permute-start.8 = (f32[16,256]{1,0:T(8,128)S(1)}, f32[16,256]{1,0:T(8,128)S(1)}, u32[]{:S(2)}, u32[]{:S(2)}) collective-permute-start(f32[16,256]{1,0:T(8,128)S(1)} %fusion), channel_id=1, source_target_pairs={{0,9},{1,10},{2,11},{3,12},{4,13},{5,14},{6,15},{7,16},{8,17},{9,1... | collective-permute-start | bytes 49160
  1976.6 23.3 %collective-permute-start.9 = (f32[16,256]{1,0:T(8,128)S(1)}, f32[16,256]{1,0:T(8,128)S(1)}, u32[]{:S(2)}, u32[]{:S(2)}) collective-permute-start(f32[16,256]{1,0:T(8,128)S(1)} %fusion), channel_id=1, source_target_pairs={{0,10},{1,11},{2,12},{3,13},{4,14},{5,15},{6,16},{7,17},{8,18},{9,... | collective-permute-start | bytes 49160
  (40 other events, 282.1 us)
Sparse Core Ops, SparseCore 0:
  9.9 417.8 all-gather.5
  429.6 77.6 all-gather.3
  845.2 280.8 all-reduce.38
where the time goes:
time: 2020 us
  blocking collectives  593 us (29%)
  starting transfers between devices  546 us (27%)
  waiting for transfers between devices  501 us (25%)
  local copies, waits for them, and re-layouts  264 us (13%)
  other arithmetic  47 us (2%)
  matrix products  26.3 us (1%)
  loops' own time  24.2 us (1%)
    unnamed x1, blocking collectives  593 us
    unnamed x65, starting transfers between devices  546 us
    all_gather x1, waiting for transfers between devices, body(): lax.all_gather(probe_modes, ('scan', 'tile'), axis=0, tiled=True)  416 us
    dynamic_update_slice x4, local copies, waits for them, and re-layouts, add_patch(): lax.dynamic_update_slice(object_total, current + gradient_piece[None], an...  180 us
    all_gather x1, waiting for transfers between devices, body(): whole_object = lax.all_gather(object_tiles, 'tile', axis=0, tiled=True)  72.6 us
  transfers between devices with their start and end apart: 67, of which 4 were waited for; matrix products, arithmetic and copies ran while one was open for 30% of the time, Pallas kernels for 0%

commit v1 on v0

v1 whole, which is shorter than its diff:
```python
import functools
import math

import jax
import jax.numpy as jnp
import numpy as np
from jax import lax
from jax.experimental import pallas as pl
from jax.experimental.pallas import tpu as pltpu
from jax.sharding import Mesh
from jax.sharding import PartitionSpec as P

AXES = ("x", "yh", "z", "yl", "c")
ROWS = 128
CUT = 64


def block_matrices(pixels):
    index = np.arange(pixels, dtype=np.int64)
    chirp = ((index[:, None] - index[None, :]) ** 2 % (2 * pixels)) * (math.pi / pixels)
    turn = (index[:, None] * index[None, :] % pixels) * (2.0 * math.pi / pixels)
    scale = 1.0 / math.sqrt(pixels)
    result = []
    for re, im in ((np.cos(chirp), np.sin(chirp)), (np.cos(turn), -np.sin(turn))):
        re, im = (re * scale).astype(jnp.bfloat16), (im * scale).astype(jnp.bfloat16)
        result.append(np.block([[re, im], [-im, re]]))
        result.append(np.block([[re, -im], [im, re]]))
    return np.stack(result)


def dot(a, b):
    return jnp.dot(a, b, preferred_element_type=jnp.float32)


def kernel(
    meta,
    mine,
    other,
    own,
    partner,
    far0,
    far1,
    cross0,
    cross1,
    amplitudes,
    matrices,
    probe_grad,
    canvas,
    probe,
    tiles,
    patch,
    patch_grad,
    wave1,
    wave2,
    tall,
    wide,
    intensity,
    probe_sem,
    tile_sem,
):
    pixels = probe_grad.shape[2] * 2
    half = pixels // 2
    modes = wave1.shape[0]
    positions = tiles.shape[0]
    core = meta[0]
    steps = [slice(i, i + ROWS) for i in range(0, pixels, ROWS)]

    def low(rows):
        return slice(rows.start + pixels, rows.stop + pixels)

    copies = (
        pltpu.make_async_copy(mine, probe.at[core], probe_sem.at[0]),
        pltpu.make_async_copy(other, probe.at[1 - core], probe_sem.at[1]),
    )
    for copy in copies:
        copy.start()
    for n in range(positions):
        kind = meta[1 + 5 * n]
        for source, (first, second) in enumerate(
            ((own.at[0], own.at[1]), (partner.at[0], partner.at[1]), (far0, far1), (cross0, cross1))
        ):

            @pl.when(kind == source)
            def _():
                pltpu.make_async_copy(first, tiles.at[n, 0], tile_sem.at[n, 0]).start()
                pltpu.make_async_copy(second, tiles.at[n, 1], tile_sem.at[n, 1]).start()

    canvas[...] = jnp.zeros_like(canvas)
    for n in range(positions):
        for k in range(2):
            pltpu.make_async_copy(far0, tiles.at[n, k], tile_sem.at[n, k]).wait()
    for copy in copies:
        copy.wait()

    def load_probe(m, part, rows):
        start = pl.multiple_of((part * modes + m) * pixels, pixels) + rows.start
        window = pl.ds(pl.multiple_of(start, ROWS), ROWS)
        return jnp.concatenate([probe[0, window, :], probe[1, window, :]], axis=1)

    def position(n, _):
        base = 1 + 5 * n
        row, down = meta[base + 1], meta[base + 2]
        column, place = meta[base + 3], meta[base + 4]
        up, back = lax.rem(CUT + 8 - down, CUT + 8), lax.rem(384 - column, 384)
        for k in range(2):
            for part in range(2):
                for i in range(0, pixels, CUT):
                    window = pl.ds(pl.multiple_of(row + i, 8), CUT + 8)
                    piece = pltpu.roll(tiles[n, k, part, window, :], up, 0)[:CUT]
                    patch[k, part, i : i + CUT, :] = pltpu.roll(piece, back, 1)[:, :pixels]
        patch_grad[...] = jnp.zeros_like(patch_grad)
        intensity[...] = jnp.zeros_like(intensity)

        def forward(m, _):
            for rows in steps:
                pr, pi = load_probe(m, 0, rows), load_probe(m, 1, rows)
                qr, qi = patch[0, 0, rows, :], patch[0, 1, rows, :]
                tall[rows, :] = (pr * qr - pi * qi).astype(jnp.bfloat16)
                tall[low(rows), :] = (pr * qi + pi * qr).astype(jnp.bfloat16)
            for rows in steps:
                wide[rows, :pixels] = dot(matrices[1, rows, :], tall[...]).astype(jnp.bfloat16)
                wide[rows, pixels:] = dot(matrices[1, low(rows), :], tall[...]).astype(jnp.bfloat16)
            for rows in steps:
                w = dot(wide[rows, :], matrices[0])
                wave1[m, rows, :] = w
                wr, wi = w[:, :pixels], w[:, pixels:]
                qr, qi = patch[1, 0, rows, :], patch[1, 1, rows, :]
                tall[rows, :] = (wr * qr - wi * qi).astype(jnp.bfloat16)
                tall[low(rows), :] = (wr * qi + wi * qr).astype(jnp.bfloat16)
            for rows in steps:
                wide[rows, :pixels] = dot(matrices[3, rows, :], tall[...]).astype(jnp.bfloat16)
                wide[rows, pixels:] = dot(matrices[3, low(rows), :], tall[...]).astype(jnp.bfloat16)
            for rows in steps:
                w = dot(wide[rows, :], matrices[2])
                wave2[m, rows, :] = w
                wr, wi = w[:, :pixels], w[:, pixels:]
                intensity[rows, :] += wr * wr + wi * wi
            return 0

        lax.fori_loop(0, modes, forward, 0)
        for rows in steps:
            measured = amplitudes[n, rows, :].astype(jnp.float32)
            intensity[rows, :] = 2.0 - 2.0 * measured * lax.rsqrt(intensity[rows, :] + 1.0)

        def backward(m, _):
            for rows in steps:
                g = intensity[rows, :]
                w = wave2[m, rows, :]
                d = (w * jnp.concatenate([g, g], axis=1)).astype(jnp.bfloat16)
                d = dot(d, matrices[3]).astype(jnp.bfloat16)
                tall[rows, :] = d[:, :pixels]
                tall[low(rows), :] = d[:, pixels:]
            for rows in steps:
                dr = dot(matrices[2, rows, :], tall[...])
                di = dot(matrices[2, low(rows), :], tall[...])
                dr = dr.astype(jnp.bfloat16).astype(jnp.float32)
                di = di.astype(jnp.bfloat16).astype(jnp.float32)
                wr, wi = wave1[m, rows, :pixels], wave1[m, rows, pixels:]
                patch_grad[1, 0, rows, :] += dr * wr + di * wi
                patch_grad[1, 1, rows, :] += di * wr - dr * wi
                qr, qi = patch[1, 0, rows, :], patch[1, 1, rows, :]
                wide[rows, :pixels] = (dr * qr + di * qi).astype(jnp.bfloat16)
                wide[rows, pixels:] = (di * qr - dr * qi).astype(jnp.bfloat16)
            for rows in steps:
                d = dot(wide[rows, :], matrices[1]).astype(jnp.bfloat16)
                tall[rows, :] = d[:, :pixels]
                tall[low(rows), :] = d[:, pixels:]
            for rows in steps:
                dr = dot(matrices[0, rows, :], tall[...])
                di = dot(matrices[0, low(rows), :], tall[...])
                dr = dr.astype(jnp.bfloat16).astype(jnp.float32)
                di = di.astype(jnp.bfloat16).astype(jnp.float32)
                pr, pi = load_probe(m, 0, rows), load_probe(m, 1, rows)
                patch_grad[0, 0, rows, :] += dr * pr + di * pi
                patch_grad[0, 1, rows, :] += di * pr - dr * pi
                qr, qi = patch[0, 0, rows, :], patch[0, 1, rows, :]
                for part, value in enumerate((dr * qr + di * qi, di * qr - dr * qi)):
                    start = pl.multiple_of((part * modes + m) * pixels, pixels) + rows.start
                    window = pl.ds(pl.multiple_of(start, ROWS), ROWS)
                    for side in range(2):
                        piece = value[:, side * half : (side + 1) * half]

                        @pl.when(n == 0)
                        def _():
                            probe_grad[side, window, :] = piece

                        @pl.when(n > 0)
                        def _():
                            probe_grad[side, window, :] += piece
            return 0

        lax.fori_loop(0, modes, backward, 0)
        for k in range(2):
            for part in range(2):
                lane = (k * 2 + part) * 320 - part * 64
                for i in range(0, pixels, CUT):
                    piece = patch_grad[k, part, i : i + CUT, :]
                    piece = jnp.pad(piece, ((0, 8), (0, 128)))
                    piece = pltpu.roll(pltpu.roll(piece, column + part * 64, 1), down, 0)
                    window = pl.ds(pl.multiple_of(row + i, 8), CUT + 8)
                    canvas[place, window, lane : lane + 384] += piece
        return 0

    lax.fori_loop(0, positions, position, 0)


def device_gradients(meta, mine, other, tile_parts, amplitudes):
    pixels = 2 * mine.shape[1]
    modes = mine.shape[0] // (2 * pixels)
    positions = amplitudes.shape[0]
    whole = pl.BlockSpec(memory_space=pltpu.VMEM)
    there = pl.BlockSpec(memory_space=pl.ANY)
    scratch = [
        pltpu.VMEM((2, mine.shape[0], half_of(pixels)), jnp.float32),
        pltpu.VMEM((positions, 2, 2, 320, 384), jnp.float32),
        pltpu.VMEM((2, 2, pixels, pixels), jnp.float32),
        pltpu.VMEM((2, 2, pixels, pixels), jnp.float32),
        pltpu.VMEM((modes, pixels, 2 * pixels), jnp.float32),
        pltpu.VMEM((modes, pixels, 2 * pixels), jnp.float32),
        pltpu.VMEM((2 * pixels, pixels), jnp.bfloat16),
        pltpu.VMEM((pixels, 2 * pixels), jnp.bfloat16),
        pltpu.VMEM((pixels, pixels), jnp.float32),
        pltpu.SemaphoreType.DMA((2,)),
        pltpu.SemaphoreType.DMA((positions, 2)),
    ]
    flops = positions * modes * 8 * 4 * 2 * pixels**3
    return pl.pallas_call(
        kernel,
        out_shape=(
            jax.ShapeDtypeStruct((2, mine.shape[0], half_of(pixels)), jnp.float32),
            jax.ShapeDtypeStruct((4, 320, 1280), jnp.float32),
        ),
        in_specs=[pl.BlockSpec(memory_space=pltpu.SMEM)] + [there] * 8 + [whole] * 2,
        out_specs=(whole, whole),
        scratch_shapes=scratch,
        cost_estimate=pl.CostEstimate(flops=flops, bytes_accessed=20_000_000, transcendentals=0),
        compiler_params=pltpu.CompilerParams(vmem_limit_bytes=56 * 1024 * 1024),
        name="gradients",
    )(meta, mine, other, *tile_parts, amplitudes, jnp.asarray(block_matrices(pixels)))


def half_of(pixels):
    return pixels // 2


def exchange(value, axes):
    return lax.all_to_all(value, axes, split_axis=0, concat_axis=0, tiled=True)


def spread(value, axes, count):
    return exchange(jnp.broadcast_to(value[None], (count,) + value.shape), axes)


def reduce_over(value, axes):
    return jnp.sum(exchange(value, axes), axis=0)


def shift(value, axes, count, by):
    return lax.ppermute(value, axes, [(i, (i + by) % count) for i in range(count)])


def body(probe_modes, object_tiles, scan_offsets, patch_tiles, amplitudes):
    core, low_y = lax.axis_index("c"), lax.axis_index("yl")
    pixels = probe_modes.shape[1]
    own_rows = probe_modes.shape[0]
    half = pixels // 2

    padded = jnp.pad(object_tiles[0], ((0, 0), (0, 0), (0, 0), (0, 64)))
    far0 = shift(padded[0], ("yh", "yl"), 4, 1)
    far1 = shift(padded[1], ("yh", "yl"), 4, 3)
    partner = shift(padded, "c", 2, 1)

    columns = jnp.stack([probe_modes[:, :half], probe_modes[:, half:]])
    pair = exchange(columns, "c").reshape(2 * own_rows, half)
    block = spread(pair, ("z", "yl"), 16).reshape(32 * own_rows, half)
    mine = spread(block, ("x", "yh"), 8).reshape(256 * own_rows, half)
    other = shift(mine, "c", 2, 1)
    cross0 = shift(far0, "c", 2, 1)
    cross1 = shift(far1, "c", 2, 1)

    tile_y, tile_core = patch_tiles // 2, patch_tiles % 2
    kind = (tile_y ^ low_y) * 2 + (tile_core ^ core)
    aligned = jnp.minimum(scan_offsets[:, 0] // 8 * 8, 56)
    down = scan_offsets[:, 0] - aligned
    entries = jnp.stack([kind, aligned, down, scan_offsets[:, 1], tile_core * 2 + tile_y], axis=1)
    meta = jnp.concatenate([core.reshape(1), entries.reshape(-1)]).astype(jnp.int32)

    probe_part, canvas = device_gradients(
        meta, mine, other, (padded, partner, far0, far1, cross0, cross1), amplitudes
    )

    canvas = reduce_over(canvas.reshape(2, 640, 1280), "c")
    canvas = reduce_over(canvas.reshape(16, 40, 1280), ("yl", "x", "yh"))
    canvas = reduce_over(canvas.reshape(8, 5, 1280), "z")
    object_gradient = canvas.reshape(5, 2, 2, 320).transpose(1, 2, 0, 3)[None]

    probe_part = reduce_over(probe_part, "c")
    probe_part = reduce_over(probe_part.reshape(8, 32 * own_rows, half), ("x", "yh"))
    probe_part = reduce_over(probe_part.reshape(16, 2 * own_rows, half), ("z", "yl"))
    columns = exchange(probe_part.reshape(2, own_rows, half), "c")
    probe_gradient = jnp.concatenate([columns[0], columns[1]], axis=1)
    return (probe_gradient, object_gradient)


def solution(mesh):
    fine = Mesh(mesh.devices.reshape(4, 2, 8, 2, 2), AXES)
    scan, tile = AXES[:3], AXES[3:]
    placed = (
        P(AXES, None),
        P(tile, None, None, None, None),
        P(AXES, None),
        P(AXES),
        P(AXES, None, None),
    )
    return jax.shard_map(
        body,
        mesh=fine,
        in_specs=placed,
        out_specs=(P(AXES, None), P(tile, None, None, scan, None)),
        check_vma=False,
    )
```

time: 2020 us -> 259 us (0.13)
  blocking collectives: 593 us -> 58.3 us
  starting transfers between devices: 546 us -> 33.8 us
  waiting for transfers between devices: 501 us -> 108 us
  local copies, waits for them, and re-layouts: 264 us -> 8.4 us
  Pallas kernels: 0 us -> 39.5 us
  other arithmetic: 47 us -> 9.12 us
  matrix products: 26.3 us -> 0 us
  loops' own time: 24.2 us -> 0 us
    unnamed x1 -> x0, blocking collectives: 593 us -> none
    unnamed x65 -> x0, starting transfers between devices: 546 us -> none
    all_gather x2 -> x0, waiting for transfers between devices: 488 us -> none  [the longest x1 416 us: body(): lax.all_gather(probe_modes, ('scan', 'tile'), axis=0, tiled=True)]
    dynamic_update_slice x4 -> x0, local copies, waits for them, and re-layouts: 180 us -> none  [add_patch(): lax.dynamic_update_slice(object_total, current + gradient_piece[None], an...]
    all_to_all x0 -> x6, waiting for transfers between devices: none -> 85.9 us  [exchange(): return lax.all_to_all(value, axes, split_axis=0, concat_axis=0, tiled=True)]
    all_to_all x0 -> x4, blocking collectives: none -> 58.3 us  [exchange(): return lax.all_to_all(value, axes, split_axis=0, concat_axis=0, tiled=True)]
    pallas_call x0 -> x1, Pallas kernels: none -> 39.5 us  [device_gradients(): pl.pallas_call(kernel, out_shape=(jax.ShapeDtypeStruct((2, mine.shape[0],...]
    all_to_all x0 -> x6, starting transfers between devices: none -> 31.3 us  [exchange(): return lax.all_to_all(value, axes, split_axis=0, concat_axis=0, tiled=True)]
  transfers between devices with their start and end apart: 67 -> 12, of which waited for: 4 -> 9; matrix products, arithmetic and copies ran while one was open for 30% -> 5% of each run, Pallas kernels for 0% -> 0%
where the time goes in v1:
time: 259 us; the launch traced here: 258 us
  waiting for transfers between devices  108 us (42%)
  blocking collectives  58.3 us (23%)
  Pallas kernels  39.5 us (15%)
  starting transfers between devices  33.8 us (13%)
  other arithmetic  9.12 us (4%)
  local copies, waits for them, and re-layouts  8.4 us (3%)
    all_to_all x6, waiting for transfers between devices, exchange(): return lax.all_to_all(value, axes, split_axis=0, concat_axis=0, tiled=True)  85.9 us
    all_to_all x4, blocking collectives, exchange(): return lax.all_to_all(value, axes, split_axis=0, concat_axis=0, tiled=True)  58.3 us
    pallas_call x1, Pallas kernels, device_gradients(): pl.pallas_call(kernel, out_shape=(jax.ShapeDtypeStruct((2, mine.shape[0],...  39.5 us
    all_to_all x6, starting transfers between devices, exchange(): return lax.all_to_all(value, axes, split_axis=0, concat_axis=0, tiled=True)  31.3 us
    ppermute x6, waiting for transfers between devices, shift(): lax.ppermute(value, axes, [(i, (i + by) % count) for i in range(count)])  21.9 us
    reduce_sum x6, other arithmetic, reduce_over(): return jnp.sum(exchange(value, axes), axis=0)  7.82 us
  transfers between devices with their start and end apart: 12, of which 9 were waited for; matrix products, arithmetic and copies ran while one was open for 5% of the time, Pallas kernels for 0%

profile of v1, /device:TPU:6, one launch (start us, length us, event | category | flops | bytes accessed | tf_op | source)
XLA Modules:
  0.0 257.7 jit_solution(12299784289700895530)
XLA Ops:
  0.6 0.7 slice_bitcast_fusion.5
  1.4 3.7 %all_to_all.50 = f32[2,12,128]{2,1,0:T(8,128)S(1)} all-to-all(f32[2,12,128]{2,1,0:T(8,128)S(1)} %pad_maximum_fusion), channel_id=1, replica_groups=mesh['x'=4,'yh'=2,'z'=8,'yl'=2,'c'=2] {'c'}, dimensions={0} | all-to-all | bytes 24576 | tf_op jit(solution)/shard_map/all_to_all | solution.py:247
  5.1 20.5 %all_to_all.51 = f32[16,24,128]{2,1,0:T(8,128)S(1)} all-to-all(f32[16,24,128]{2,1,0:T(8,128)S(1)} %broadcast_in_dim.18), channel_id=1, replica_groups=mesh['x'=4,'yh'=2,'z'=8,'yl'=2,'c'=2] {'z','yl'}, dimensions={0} | all-to-all | bytes 393216 | tf_op jit(solution)/shard_map/all_to_all | solution.py:247
  25.6 1.3 broadcast_in_dim.20
  26.8 7.2 %all-to-all-start.2 = ((f32[8,384,128]{2,1,0:T(8,128)}), f32[8,384,128]{2,1,0:T(8,128)S(1)}, u32[]{:S(2)}, u32[]{:S(2)}) async-start(f32[8,384,128]{2,1,0:T(8,128)} %broadcast_in_dim.20), calls=%async_computation.2 | async-start | bytes 3145728 | tf_op jit(solution)/shard_map/all_to_all | solution.py:247
  34.1 1.4 slice_bitcast_fusion
  35.5 2.4 collective-permute-start.3
  37.9 0.0 collective-permute-start.2
  37.9 1.4 pad.4.own
  39.3 0.0 collective-permute-start.1
  39.4 14.5 %all-to-all-done.2 = f32[8,384,128]{2,1,0:T(8,128)S(1)} async-done(((f32[8,384,128]{2,1,0:T(8,128)}), f32[8,384,128]{2,1,0:T(8,128)S(1)}, u32[]{:S(2)}, u32[]{:S(2)}) %all-to-all-start.2) | async-done | bytes 1572896 | tf_op jit(solution)/shard_map/all_to_all | solution.py:247
  53.8 0.0 collective-permute-start
  53.8 16.6 %collective-permute-done.3.far1 = f32[2,320,384]{2,1,0:T(8,128)} collective-permute-done((f32[2,320,384]{2,1,0:T(8,128)}, f32[2,320,384]{2,1,0:T(8,128)}, u32[]{:S(2)}, u32[]{:S(2)}) %collective-permute-start.3) | collective-permute-done | bytes 983072 | tf_op jit(solution)/shard_map/ppermute | solution.py:259
  70.5 0.0 collective-permute-start.5
  70.5 3.5 %collective-permute-done.2.far0 = f32[2,320,384]{2,1,0:T(8,128)} collective-permute-done((f32[2,320,384]{2,1,0:T(8,128)}, f32[2,320,384]{2,1,0:T(8,128)}, u32[]{:S(2)}, u32[]{:S(2)}) %collective-permute-start.2) | collective-permute-done | bytes 983072 | tf_op jit(solution)/shard_map/ppermute | solution.py:259
  74.0 0.0 collective-permute-start.4
  74.0 0.1 copy.18
  74.1 0.1 copy.19
  74.2 0.1 slice_subtract_fusion
  74.3 0.1 stack.22
  74.4 0.1 reshape.37
  74.5 0.6 pad_add_fusion.meta
  75.1 0.0 collective-permute-done.5.cross1
  75.1 1.8 collective-permute-done.4.cross0
  76.9 0.0 collective-permute-done.1.partner
  76.9 1.1 copy-done.4
  78.0 39.5 %gradients.1 = (f32[2,3072,128]{2,1,0:T(8,128)}, f32[4,320,1280]{2,1,0:T(8,128)}) custom-call(s32[11]{0:T(128)} %pad_add_fusion.meta, f32[3072,128]{1,0:T(8,128)} %bitcast.33, f32[3072,128]{1,0:T(8,128)} %copy-done.4, f32[2,2,320,384]{3,2,1,0:T(8,128)} %pad.4.own, f32[2,2,320,384]{3,2,1,0:T(8,128)} %collective-permute-done.1.partner, ...), custom_call_target="tpu_custom_call" | custom-call | flops 12884901888 | bytes 20000000 | tf_op jit(solution)/shard_map/gradients/pallas_call | solution.py:227
  117.5 7.6 %all_to_all.52 = f32[2,3072,128]{2,1,0:T(8,128)S(1)} all-to-all(f32[2,3072,128]{2,1,0:T(8,128)} %get-tuple-element.4), channel_id=1, replica_groups=mesh['x'=4,'yh'=2,'z'=8,'yl'=2,'c'=2] {'c'}, dimensions={0} | all-to-all | bytes 6291456 | tf_op jit(solution)/shard_map/all_to_all | solution.py:247
  125.1 1.5 reduce_sum.54
  126.6 26.6 %all_to_all.53 = f32[8,384,128]{2,1,0:T(8,128)S(1)} all-to-all(f32[8,384,128]{2,1,0:T(8,128)} %bitcast.31), channel_id=1, replica_groups=mesh['x'=4,'yh'=2,'z'=8,'yl'=2,'c'=2] {'x','yh'}, dimensions={0} | all-to-all | bytes 3145728 | tf_op jit(solution)/shard_map/all_to_all | solution.py:247
  153.2 6.4 %all-to-all-start.7 = ((f32[2,640,1280]{2,1,0:T(8,128)}), f32[2,640,1280]{2,1,0:T(8,128)}, u32[]{:S(2)}, u32[]{:S(2)}) async-start(f32[2,640,1280]{2,1,0:T(8,128)} %bitcast.30), calls=%async_computation.7 | async-start | bytes 13107200 | tf_op jit(solution)/shard_map/all_to_all | solution.py:247
  159.6 0.8 reduce_sum.55
  160.4 5.4 %all-to-all-done.7 = f32[2,640,1280]{2,1,0:T(8,128)} async-done(((f32[2,640,1280]{2,1,0:T(8,128)}), f32[2,640,1280]{2,1,0:T(8,128)}, u32[]{:S(2)}, u32[]{:S(2)}) %all-to-all-start.7) | async-done | bytes 6553632 | tf_op jit(solution)/shard_map/all_to_all | solution.py:247
  165.8 3.6 %all-to-all-start.5 = ((f32[16,24,128]{2,1,0:T(8,128)}), f32[16,24,128]{2,1,0:T(8,128)S(1)}, u32[]{:S(2)}, u32[]{:S(2)}) async-start(f32[16,24,128]{2,1,0:T(8,128)} %bitcast.11), calls=%async_computation.5 | async-start | bytes 393216 | tf_op jit(solution)/shard_map/all_to_all | solution.py:247
  169.4 5.3 %reduce_sum.57 = f32[640,1280]{1,0:T(8,128)} reduce(f32[2,640,1280]{2,1,0:T(8,128)} %all-to-all-done.7, f32[]{:T(128)} %constant.53.clone.1), dimensions={0}, to_apply=%region_3.4 | reduce | flops 819200 | bytes 9830404 | tf_op jit(solution)/shard_map/reduce_sum | solution.py:255
  174.7 6.2 %all-to-all-done.5 = f32[16,24,128]{2,1,0:T(8,128)S(1)} async-done(((f32[16,24,128]{2,1,0:T(8,128)}), f32[16,24,128]{2,1,0:T(8,128)S(1)}, u32[]{:S(2)}, u32[]{:S(2)}) %all-to-all-start.5) | async-done | bytes 196640 | tf_op jit(solution)/shard_map/all_to_all | solution.py:247
  181.0 5.8 %all-to-all-start.8 = ((f32[16,40,1280]{2,1,0:T(8,128)}), f32[16,40,1280]{2,1,0:T(8,128)S(1)}, u32[]{:S(2)}, u32[]{:S(2)}) async-start(f32[16,40,1280]{2,1,0:T(8,128)} %bitcast.27), calls=%async_computation.8 | async-start | bytes 6553600 | tf_op jit(solution)/shard_map/all_to_all | solution.py:247
  186.8 0.6 reshape.41
  187.4 46.3 %all-to-all-done.8 = f32[16,40,1280]{2,1,0:T(8,128)S(1)} async-done(((f32[16,40,1280]{2,1,0:T(8,128)}), f32[16,40,1280]{2,1,0:T(8,128)S(1)}, u32[]{:S(2)}, u32[]{:S(2)}) %all-to-all-start.8) | async-done | bytes 3276832 | tf_op jit(solution)/shard_map/all_to_all | solution.py:247
  233.7 3.2 %all-to-all-start.6 = ((f32[2,12,128]{2,1,0:T(8,128)}), f32[2,12,128]{2,1,0:T(8,128)S(1)}, u32[]{:S(2)}, u32[]{:S(2)}) async-start(f32[2,12,128]{2,1,0:T(8,128)} %reshape.41), calls=%async_computation.6 | async-start | bytes 32768 | tf_op jit(solution)/shard_map/all_to_all | solution.py:247
  237.0 0.2 reduce_sum.58
  237.1 0.8 reshape.44
  237.9 0.4 all-to-all-done.6
  238.3 5.0 %all-to-all-start.9 = ((f32[8,5,1280]{2,1,0:T(8,128)}), f32[8,5,1280]{2,1,0:T(8,128)S(1)}, u32[]{:S(2)}, u32[]{:S(2)}) async-start(f32[8,5,1280]{2,1,0:T(8,128)} %reshape.44), calls=%async_computation.9 | async-start | bytes 655360 | tf_op jit(solution)/shard_map/all_to_all | solution.py:247
  243.3 0.6 pad_maximum_fusion.1
  243.9 13.0 %all-to-all-done.9 = f32[8,5,1280]{2,1,0:T(8,128)S(1)} async-done(((f32[8,5,1280]{2,1,0:T(8,128)}), f32[8,5,1280]{2,1,0:T(8,128)S(1)}, u32[]{:S(2)}, u32[]{:S(2)}) %all-to-all-start.9) | async-done | bytes 204832 | tf_op jit(solution)/shard_map/all_to_all | solution.py:247
  257.0 0.1 reshape.45
  257.1 0.6 copy.20
  (18 shorter events, 0.1 us)
Async XLA Ops:
  26.8 7.2 %copy-start = (f32[1,2,2,320,320]{4,3,2,1,0:T(8,128)S(1)}, f32[1,2,2,320,320]{4,3,2,1,0:T(8,128)}, u32[]{:S(2)}) copy-start(f32[1,2,2,320,320]{4,3,2,1,0:T(8,128)} %param.7) | copy-start | bytes 4915204
  26.8 27.0 %all-to-all-start.2 = ((f32[8,384,128]{2,1,0:T(8,128)}), f32[8,384,128]{2,1,0:T(8,128)S(1)}, u32[]{:S(2)}, u32[]{:S(2)}) async-start(f32[8,384,128]{2,1,0:T(8,128)} %broadcast_in_dim.20), calls=%async_computation.2 | async-start | bytes 3145728 | tf_op jit(solution)/shard_map/all_to_all | solution.py:247
  35.5 35.0 %collective-permute-start.3 = (f32[2,320,384]{2,1,0:T(8,128)}, f32[2,320,384]{2,1,0:T(8,128)}, u32[]{:S(2)}, u32[]{:S(2)}) collective-permute-start(f32[2,320,384]{2,1,0:T(8,128)} %get-tuple-element.17), channel_id=1, source_target_pairs={{0,34},{2,0},{32,2},{34,32},{1,35},{3,1},{33,3},{35,33},{4,38},{6,... | collective-permute-start | bytes 2949128 | tf_op jit(solution)/shard_map/ppermute | solution.py:259
  37.9 36.1 %copy-start.3 = (s32[2]{0:T(128)S(1)}, s32[2]{0:T(128)}, u32[]{:S(2)}) copy-start(s32[2]{0:T(128)} %param.9) | copy-start | bytes 28
  37.9 36.3 %copy-start.2 = (s32[2,2]{1,0:T(2,128)S(1)}, s32[2,2]{1,0:T(2,128)}, u32[]{:S(2)}) copy-start(s32[2,2]{1,0:T(2,128)} %param.8) | copy-start | bytes 52
  37.9 36.0 %collective-permute-start.2 = (f32[2,320,384]{2,1,0:T(8,128)}, f32[2,320,384]{2,1,0:T(8,128)}, u32[]{:S(2)}, u32[]{:S(2)}) collective-permute-start(f32[2,320,384]{2,1,0:T(8,128)} %get-tuple-element.18), channel_id=1, source_target_pairs={{0,2},{2,32},{32,34},{34,0},{1,3},{3,33},{33,35},{35,1},{4,6},{6,3... | collective-permute-start | bytes 2949128 | tf_op jit(solution)/shard_map/ppermute | solution.py:259
  39.3 37.5 %collective-permute-start.1 = (f32[2,2,320,384]{3,2,1,0:T(8,128)}, f32[2,2,320,384]{3,2,1,0:T(8,128)}, u32[]{:S(2)}, u32[]{:S(2)}) collective-permute-start(f32[2,2,320,384]{3,2,1,0:T(8,128)} %pad.4.own), channel_id=1, source_target_pairs={{0,1},{1,0},{2,3},{3,2},{4,5},{5,4},{6,7},{7,6},{8,9},{9,8},{10,11... | collective-permute-start | bytes 5898248 | tf_op jit(solution)/shard_map/ppermute | solution.py:259
  53.8 23.1 %copy-start.1 = (f32[8,384,128]{2,1,0:T(8,128)}, f32[8,384,128]{2,1,0:T(8,128)S(1)}, u32[]{:S(2)}) copy-start(f32[8,384,128]{2,1,0:T(8,128)S(1)} %all-to-all-done.2) | copy-start | bytes 4718596
  53.8 23.0 %collective-permute-start = (f32[3072,128]{1,0:T(8,128)S(1)}, f32[3072,128]{1,0:T(8,128)S(1)}, u32[]{:S(2)}, u32[]{:S(2)}) collective-permute-start(f32[3072,128]{1,0:T(8,128)S(1)} %bitcast.32), channel_id=1, source_target_pairs={{0,1},{1,0},{2,3},{3,2},{4,5},{5,4},{6,7},{7,6},{8,9},{9,8},{10,11... | collective-permute-start | bytes 4718600 | tf_op jit(solution)/shard_map/ppermute | solution.py:259
  70.5 4.6 %collective-permute-start.5 = (f32[2,320,384]{2,1,0:T(8,128)}, f32[2,320,384]{2,1,0:T(8,128)}, u32[]{:S(2)}, u32[]{:S(2)}) collective-permute-start(f32[2,320,384]{2,1,0:T(8,128)} %collective-permute-done.3.far1), channel_id=1, source_target_pairs={{0,1},{1,0},{2,3},{3,2},{4,5},{5,4},{6,7},{7,6},{8,9},{9,8},{10,11... | collective-permute-start | bytes 2949128 | tf_op jit(solution)/shard_map/ppermute | solution.py:259
  74.0 2.9 %collective-permute-start.4 = (f32[2,320,384]{2,1,0:T(8,128)}, f32[2,320,384]{2,1,0:T(8,128)}, u32[]{:S(2)}, u32[]{:S(2)}) collective-permute-start(f32[2,320,384]{2,1,0:T(8,128)} %collective-permute-done.2.far0), channel_id=1, source_target_pairs={{0,1},{1,0},{2,3},{3,2},{4,5},{5,4},{6,7},{7,6},{8,9},{9,8},{10,11... | collective-permute-start | bytes 2949128 | tf_op jit(solution)/shard_map/ppermute | solution.py:259
  76.9 1.1 copy-start.4
  153.2 12.6 %all-to-all-start.7 = ((f32[2,640,1280]{2,1,0:T(8,128)}), f32[2,640,1280]{2,1,0:T(8,128)}, u32[]{:S(2)}, u32[]{:S(2)}) async-start(f32[2,640,1280]{2,1,0:T(8,128)} %bitcast.30), calls=%async_computation.7 | async-start | bytes 13107200 | tf_op jit(solution)/shard_map/all_to_all | solution.py:247
  165.8 15.2 %all-to-all-start.5 = ((f32[16,24,128]{2,1,0:T(8,128)}), f32[16,24,128]{2,1,0:T(8,128)S(1)}, u32[]{:S(2)}, u32[]{:S(2)}) async-start(f32[16,24,128]{2,1,0:T(8,128)} %bitcast.11), calls=%async_computation.5 | async-start | bytes 393216 | tf_op jit(solution)/shard_map/all_to_all | solution.py:247
  181.0 52.8 %all-to-all-start.8 = ((f32[16,40,1280]{2,1,0:T(8,128)}), f32[16,40,1280]{2,1,0:T(8,128)S(1)}, u32[]{:S(2)}, u32[]{:S(2)}) async-start(f32[16,40,1280]{2,1,0:T(8,128)} %bitcast.27), calls=%async_computation.8 | async-start | bytes 6553600 | tf_op jit(solution)/shard_map/all_to_all | solution.py:247
  233.7 4.6 %all-to-all-start.6 = ((f32[2,12,128]{2,1,0:T(8,128)}), f32[2,12,128]{2,1,0:T(8,128)S(1)}, u32[]{:S(2)}, u32[]{:S(2)}) async-start(f32[2,12,128]{2,1,0:T(8,128)} %reshape.41), calls=%async_computation.6 | async-start | bytes 32768 | tf_op jit(solution)/shard_map/all_to_all | solution.py:247
  238.3 18.6 %all-to-all-start.9 = ((f32[8,5,1280]{2,1,0:T(8,128)}), f32[8,5,1280]{2,1,0:T(8,128)S(1)}, u32[]{:S(2)}, u32[]{:S(2)}) async-start(f32[8,5,1280]{2,1,0:T(8,128)} %reshape.44), calls=%async_computation.9 | async-start | bytes 655360 | tf_op jit(solution)/shard_map/all_to_all | solution.py:247

commit v2 on v1

--- a/solution.py
+++ b/solution.py
@@ -1,4 +1,3 @@
-import functools
 import math
 
 import jax
@@ -44,6 +43,8 @@
     cross1,
     amplitudes,
     matrices,
+    keep,
+    send,
     probe_grad,
     canvas,
     probe,
@@ -57,6 +58,7 @@
     intensity,
     probe_sem,
     tile_sem,
+    out_sem,
 ):
     pixels = probe_grad.shape[2] * 2
     half = pixels // 2
@@ -68,12 +70,36 @@
     def low(rows):
         return slice(rows.start + pixels, rows.stop + pixels)
 
-    copies = (
-        pltpu.make_async_copy(mine, probe.at[core], probe_sem.at[0]),
-        pltpu.make_async_copy(other, probe.at[1 - core], probe_sem.at[1]),
-    )
+    blocks = probe.reshape(2, 8, 8, 2, 24, half)
+    copies = [
+        pltpu.make_async_copy(source.at[:, y], blocks.at[side, :, :, y], probe_sem.at[i, y])
+        for i, (source, side) in enumerate(((mine, core), (other, 1 - core)))
+        for y in range(2)
+    ]
     for copy in copies:
         copy.start()
+    grad_blocks = probe_grad.reshape(2, 8, 8, 2, 24, half)
+    probe_out = [
+        pltpu.make_async_copy(
+            grad_blocks.at[side, :, z, y],
+            target.at[8 * y : 8 * y + 8, 400 + 24 * z : 424 + 24 * z, :],
+            out_sem.at[i, y, z],
+        )
+        for i, (target, side) in enumerate(((keep, core), (send, 1 - core)))
+        for y in range(2)
+        for z in range(8)
+    ]
+    canvas_blocks = canvas.reshape(4, 8, 40, 1280)
+    canvas_out = [
+        pltpu.make_async_copy(
+            canvas_blocks.at[2 * i + y, :, :, 128 * j : 128 * j + 128],
+            target.at[8 * y : 8 * y + 8, 40 * j : 40 * j + 40, :],
+            out_sem.at[i, y, 8 + j],
+        )
+        for i, target in enumerate((keep, send))
+        for y in range(2)
+        for j in range(10)
+    ]
     for n in range(positions):
         kind = meta[1 + 5 * n]
         for source, (first, second) in enumerate(
@@ -190,6 +216,12 @@
             return 0
 
         lax.fori_loop(0, modes, backward, 0)
+
+        @pl.when(n == positions - 1)
+        def _():
+            for copy in probe_out:
+                copy.start()
+
         for k in range(2):
             for part in range(2):
                 lane = (k * 2 + part) * 320 - part * 64
@@ -202,16 +234,23 @@
         return 0
 
     lax.fori_loop(0, positions, position, 0)
+    for copy in canvas_out:
+        copy.start()
+    for copy in probe_out + canvas_out:
+        copy.wait()
 
 
 def device_gradients(meta, mine, other, tile_parts, amplitudes):
-    pixels = 2 * mine.shape[1]
-    modes = mine.shape[0] // (2 * pixels)
+    pixels = 2 * mine.shape[-1]
+    rows = math.prod(mine.shape[:-1])
+    modes = rows // (2 * pixels)
     positions = amplitudes.shape[0]
     whole = pl.BlockSpec(memory_space=pltpu.VMEM)
     there = pl.BlockSpec(memory_space=pl.ANY)
     scratch = [
-        pltpu.VMEM((2, mine.shape[0], half_of(pixels)), jnp.float32),
+        pltpu.VMEM((2, rows, pixels // 2), jnp.float32),
+        pltpu.VMEM((4, 320, 1280), jnp.float32),
+        pltpu.VMEM((2, rows, pixels // 2), jnp.float32),
         pltpu.VMEM((positions, 2, 2, 320, 384), jnp.float32),
         pltpu.VMEM((2, 2, pixels, pixels), jnp.float32),
         pltpu.VMEM((2, 2, pixels, pixels), jnp.float32),
@@ -220,18 +259,16 @@
         pltpu.VMEM((2 * pixels, pixels), jnp.bfloat16),
         pltpu.VMEM((pixels, 2 * pixels), jnp.bfloat16),
         pltpu.VMEM((pixels, pixels), jnp.float32),
-        pltpu.SemaphoreType.DMA((2,)),
+        pltpu.SemaphoreType.DMA((2, 2)),
         pltpu.SemaphoreType.DMA((positions, 2)),
+        pltpu.SemaphoreType.DMA((2, 2, 18)),
     ]
     flops = positions * modes * 8 * 4 * 2 * pixels**3
     return pl.pallas_call(
         kernel,
-        out_shape=(
-            jax.ShapeDtypeStruct((2, mine.shape[0], half_of(pixels)), jnp.float32),
-            jax.ShapeDtypeStruct((4, 320, 1280), jnp.float32),
-        ),
+        out_shape=(jax.ShapeDtypeStruct((16, 592, 128), jnp.float32),) * 2,
         in_specs=[pl.BlockSpec(memory_space=pltpu.SMEM)] + [there] * 8 + [whole] * 2,
-        out_specs=(whole, whole),
+        out_specs=(there, there),
         scratch_shapes=scratch,
         cost_estimate=pl.CostEstimate(flops=flops, bytes_accessed=20_000_000, transcendentals=0),
         compiler_params=pltpu.CompilerParams(vmem_limit_bytes=56 * 1024 * 1024),
@@ -239,10 +276,6 @@
     )(meta, mine, other, *tile_parts, amplitudes, jnp.asarray(block_matrices(pixels)))
 
 
-def half_of(pixels):
-    return pixels // 2
-
-
 def exchange(value, axes):
     return lax.all_to_all(value, axes, split_axis=0, concat_axis=0, tiled=True)
 
@@ -259,45 +292,43 @@
     return lax.ppermute(value, axes, [(i, (i + by) % count) for i in range(count)])
 
 
-def body(probe_modes, object_tiles, scan_offsets, patch_tiles, amplitudes):
+def device_body(probe_modes, object_tiles, scan_offsets, patch_tiles, amplitudes):
     core, low_y = lax.axis_index("c"), lax.axis_index("yl")
-    pixels = probe_modes.shape[1]
-    own_rows = probe_modes.shape[0]
+    own_rows, pixels = probe_modes.shape
     half = pixels // 2
 
     padded = jnp.pad(object_tiles[0], ((0, 0), (0, 0), (0, 0), (0, 64)))
     far0 = shift(padded[0], ("yh", "yl"), 4, 1)
     far1 = shift(padded[1], ("yh", "yl"), 4, 3)
     partner = shift(padded, "c", 2, 1)
+    cross0 = shift(far0, "c", 2, 1)
+    cross1 = shift(far1, "c", 2, 1)
 
     columns = jnp.stack([probe_modes[:, :half], probe_modes[:, half:]])
     pair = exchange(columns, "c").reshape(2 * own_rows, half)
-    block = spread(pair, ("z", "yl"), 16).reshape(32 * own_rows, half)
-    mine = spread(block, ("x", "yh"), 8).reshape(256 * own_rows, half)
+    block = spread(pair, "z", 8)
+    mine = spread(block, ("x", "yh", "yl"), 16).reshape(8, 2, 8, 2 * own_rows, half)
     other = shift(mine, "c", 2, 1)
-    cross0 = shift(far0, "c", 2, 1)
-    cross1 = shift(far1, "c", 2, 1)
 
     tile_y, tile_core = patch_tiles // 2, patch_tiles % 2
-    kind = (tile_y ^ low_y) * 2 + (tile_core ^ core)
+    kind = (tile_core ^ core) + 2 * (tile_y ^ low_y)
     aligned = jnp.minimum(scan_offsets[:, 0] // 8 * 8, 56)
     down = scan_offsets[:, 0] - aligned
-    entries = jnp.stack([kind, aligned, down, scan_offsets[:, 1], tile_core * 2 + tile_y], axis=1)
+    place = 2 * (tile_core ^ core) + tile_y
+    entries = jnp.stack([kind, aligned, down, scan_offsets[:, 1], place], axis=1)
     meta = jnp.concatenate([core.reshape(1), entries.reshape(-1)]).astype(jnp.int32)
 
-    probe_part, canvas = device_gradients(
+    keep, send = device_gradients(
         meta, mine, other, (padded, partner, far0, far1, cross0, cross1), amplitudes
     )
 
-    canvas = reduce_over(canvas.reshape(2, 640, 1280), "c")
-    canvas = reduce_over(canvas.reshape(16, 40, 1280), ("yl", "x", "yh"))
-    canvas = reduce_over(canvas.reshape(8, 5, 1280), "z")
-    object_gradient = canvas.reshape(5, 2, 2, 320).transpose(1, 2, 0, 3)[None]
-
-    probe_part = reduce_over(probe_part, "c")
-    probe_part = reduce_over(probe_part.reshape(8, 32 * own_rows, half), ("x", "yh"))
-    probe_part = reduce_over(probe_part.reshape(16, 2 * own_rows, half), ("z", "yl"))
-    columns = exchange(probe_part.reshape(2, own_rows, half), "c")
+    total = keep + shift(send, "c", 2, 1)
+    total = reduce_over(total, ("yl", "x", "yh"))
+    objects = total[:400].reshape(10, 8, 5, 128).transpose(1, 0, 2, 3).reshape(8, 50, 128)
+    total = reduce_over(jnp.concatenate([objects, total[400:].reshape(8, 24, 128)], axis=1), "z")
+    object_gradient = total[:50].reshape(10, 5, 128).transpose(1, 0, 2).reshape(5, 2, 2, 320)
+    object_gradient = object_gradient.transpose(1, 2, 0, 3)[None]
+    columns = exchange(total[50:].reshape(2, own_rows, half), "c")
     probe_gradient = jnp.concatenate([columns[0], columns[1]], axis=1)
     return (probe_gradient, object_gradient)
 
@@ -313,7 +344,7 @@
         P(AXES, None, None),
     )
     return jax.shard_map(
-        body,
+        device_body,
         mesh=fine,
         in_specs=placed,
         out_specs=(P(AXES, None), P(tile, None, None, scan, None)),

time: 259 us -> 217 us (0.84)
  waiting for transfers between devices: 108 us -> 45.1 us
  blocking collectives: 58.3 us -> 99.4 us
  starting transfers between devices: 33.8 us -> 13.6 us
    all_to_all x6 -> x2, waiting for transfers between devices: 85.9 us -> 15.1 us  [exchange(): return lax.all_to_all(value, axes, split_axis=0, concat_axis=0, tiled=True)]
    all_to_all x4, blocking collectives: 58.3 us -> 99.4 us  [exchange(): return lax.all_to_all(value, axes, split_axis=0, concat_axis=0, tiled=True)]
    all_to_all x6 -> x2, starting transfers between devices: 31.3 us -> 10.8 us  [exchange(): return lax.all_to_all(value, axes, split_axis=0, concat_axis=0, tiled=True)]
    ppermute x6 -> x7, waiting for transfers between devices: 21.9 us -> 30 us  [shift(): lax.ppermute(value, axes, [(i, (i + by) % count) for i in range(count)])]
    reduce_sum x6 -> x2, other arithmetic: 7.82 us -> 2.65 us  [reduce_over(): return jnp.sum(exchange(value, axes), axis=0)]
    add x0 -> x1, other arithmetic: none -> 2.86 us  [device_body(): total = keep + shift(send, 'c', 2, 1)]
  transfers between devices with their start and end apart: 12 -> 9, of which waited for: 9 -> 7; matrix products, arithmetic and copies ran while one was open for 5% -> 2% of each run, Pallas kernels for 0% -> 0%
where the time goes in v2:
time: 217 us; the launch traced here: 213 us
  blocking collectives  99.4 us (46%)
  waiting for transfers between devices  45.1 us (21%)
  Pallas kernels  39.8 us (18%)
  starting transfers between devices  13.6 us (6%)
  local copies, waits for them, and re-layouts  7.96 us (4%)
  other arithmetic  6.83 us (3%)
    all_to_all x4, blocking collectives, exchange(): return lax.all_to_all(value, axes, split_axis=0, concat_axis=0, tiled=True)  99.4 us
    pallas_call x1, Pallas kernels, device_gradients(): pl.pallas_call(kernel, out_shape=(jax.ShapeDtypeStruct((16, 592, 128), jn...  39.8 us
    ppermute x7, waiting for transfers between devices, shift(): lax.ppermute(value, axes, [(i, (i + by) % count) for i in range(count)])  30 us
    all_to_all x2, waiting for transfers between devices, exchange(): return lax.all_to_all(value, axes, split_axis=0, concat_axis=0, tiled=True)  15.1 us
    all_to_all x2, starting transfers between devices, exchange(): return lax.all_to_all(value, axes, split_axis=0, concat_axis=0, tiled=True)  10.8 us
  transfers between devices with their start and end apart: 9, of which 7 were waited for; matrix products, arithmetic and copies ran while one was open for 2% of the time, Pallas kernels for 0%

profile of v2, /device:TPU:6, one launch (start us, length us, event | category | flops | bytes accessed | tf_op | source)
XLA Modules:
  0.0 213.5 jit_solution(14713682211423163943)
XLA Ops:
  0.6 0.7 slice_bitcast_fusion.5
  1.4 3.7 %all_to_all.30 = f32[2,12,128]{2,1,0:T(8,128)S(1)} all-to-all(f32[2,12,128]{2,1,0:T(8,128)S(1)} %pad_maximum_fusion.1), channel_id=1, replica_groups=mesh['x'=4,'yh'=2,'z'=8,'yl'=2,'c'=2] {'c'}, dimensions={0} | all-to-all | bytes 24576 | tf_op jit(solution)/shard_map/all_to_all | solution.py:280
  5.1 17.1 %all_to_all.31 = f32[8,24,128]{2,1,0:T(8,128)S(1)} all-to-all(f32[8,24,128]{2,1,0:T(8,128)S(1)} %broadcast_in_dim.17), channel_id=1, replica_groups=mesh['x'=4,'yh'=2,'z'=8,'yl'=2,'c'=2] {'z'}, dimensions={0} | all-to-all | bytes 196608 | tf_op jit(solution)/shard_map/all_to_all | solution.py:280
  22.2 1.3 broadcast_in_dim.18
  23.5 0.0 copy-start
  23.5 7.6 %all-to-all-start.2 = ((f32[16,8,24,128]{3,2,1,0:T(8,128)}), f32[16,8,24,128]{3,2,1,0:T(8,128)S(1)}, u32[]{:S(2)}, u32[]{:S(2)}) async-start(f32[16,8,24,128]{3,2,1,0:T(8,128)} %broadcast_in_dim.18), calls=%async_computation.2 | async-start | bytes 3145728 | tf_op jit(solution)/shard_map/all_to_all | solution.py:280
  31.1 0.0 copy-done
  31.1 1.4 slice_bitcast_fusion
  32.5 2.7 %collective-permute-start.3 = (f32[2,320,384]{2,1,0:T(8,128)}, f32[2,320,384]{2,1,0:T(8,128)}, u32[]{:S(2)}, u32[]{:S(2)}) collective-permute-start(f32[2,320,384]{2,1,0:T(8,128)} %get-tuple-element.17), channel_id=1, source_target_pairs={{0,34},{2,0},{32,2},{34,32},{1,35},{3,1},{33,3},{35,33},{4,38},{6,... | collective-permute-start | bytes 2949128 | tf_op jit(solution)/shard_map/ppermute | solution.py:292
  35.2 0.0 copy-start.3
  35.2 0.0 collective-permute-start.2
  35.2 1.4 pad.4.own
  36.6 0.0 collective-permute-start.1
  36.6 14.5 %all-to-all-done.2 = f32[16,8,24,128]{3,2,1,0:T(8,128)S(1)} async-done(((f32[16,8,24,128]{3,2,1,0:T(8,128)}), f32[16,8,24,128]{3,2,1,0:T(8,128)S(1)}, u32[]{:S(2)}, u32[]{:S(2)}) %all-to-all-start.2) | async-done | bytes 1572896 | tf_op jit(solution)/shard_map/all_to_all | solution.py:280
  51.1 0.0 collective-permute-start
  51.1 18.5 %collective-permute-done.3.far1 = f32[2,320,384]{2,1,0:T(8,128)} collective-permute-done((f32[2,320,384]{2,1,0:T(8,128)}, f32[2,320,384]{2,1,0:T(8,128)}, u32[]{:S(2)}, u32[]{:S(2)}) %collective-permute-start.3) | collective-permute-done | bytes 983072 | tf_op jit(solution)/shard_map/ppermute | solution.py:292
  69.6 0.0 collective-permute-start.5
  69.6 1.2 collective-permute-done.2.far0
  70.8 0.0 collective-permute-start.4
  70.8 0.0 copy-done.3
  70.8 0.1 copy.23
  70.9 0.1 copy.24
  71.0 0.0 copy-done.2
  71.0 0.1 slice_subtract_fusion
  71.1 0.1 stack.22
  71.2 0.1 reshape.34
  71.2 0.6 pad_add_fusion.meta
  71.8 0.7 collective-permute-done.5.cross1
  72.5 1.4 collective-permute-done.4.cross0
  73.9 0.0 collective-permute-done.1.partner
  73.9 0.0 collective-permute-done.other
  73.9 0.0 copy-done.1
  73.9 0.0 copy-start.4
  73.9 1.1 copy-done.4
  75.1 39.8 %gradients.1 = (f32[16,592,128]{2,1,0:T(8,128)}, f32[16,592,128]{2,1,0:T(8,128)}) custom-call(s32[11]{0:T(128)} %pad_add_fusion.meta, f32[8,2,8,24,128]{4,3,2,1,0:T(8,128)} %bitcast.29, f32[8,2,8,24,128]{4,3,2,1,0:T(8,128)} %copy-done.4, f32[2,2,320,384]{3,2,1,0:T(8,128)} %pad.4.own, f32[2,2,320,384]{3,2,1,0:T(8,128)} %collective-permute-done.1.partner, ...), custom_call_target="tpu_custom_call" | custom-call | flops 12884901888 | bytes 20000000 | tf_op jit(solution)/shard_map/gradients/pallas_call | solution.py:267
  114.9 0.1 collective-permute-start.6
  115.0 8.3 %collective-permute-done.6 = f32[16,592,128]{2,1,0:T(8,128)S(1)} collective-permute-done((f32[16,592,128]{2,1,0:T(8,128)}, f32[16,592,128]{2,1,0:T(8,128)S(1)}, u32[]{:S(2)}, u32[]{:S(2)}) %collective-permute-start.6) | collective-permute-done | bytes 4849696 | tf_op jit(solution)/shard_map/ppermute | solution.py:292
  123.3 2.9 %add.24 = f32[16,592,128]{2,1,0:T(8,128)S(1)} add(f32[16,592,128]{2,1,0:T(8,128)} %get-tuple-element.4, f32[16,592,128]{2,1,0:T(8,128)S(1)} %collective-permute-done.6) | non-fusion elementwise | flops 1212416 | bytes 14548992 | tf_op jit(solution)/shard_map/add | solution.py:325
  126.1 63.4 %all_to_all.32 = f32[16,592,128]{2,1,0:T(8,128)} all-to-all(f32[16,592,128]{2,1,0:T(8,128)S(1)} %add.24), channel_id=1, replica_groups=mesh['x'=4,'yh'=2,'z'=8,'yl'=2,'c'=2] {'yl','x','yh'}, dimensions={0} | all-to-all | bytes 9699328 | tf_op jit(solution)/shard_map/all_to_all | solution.py:280
  189.5 2.6 %reduce_sum.18 = f32[592,128]{1,0:T(8,128)S(1)} reduce(f32[16,592,128]{2,1,0:T(8,128)} %all_to_all.32, f32[]{:T(128)} %constant.53.clone.1), dimensions={0}, to_apply=%region_0.1 | reduce | flops 1136640 | bytes 5152772 | tf_op jit(solution)/shard_map/reduce_sum | solution.py:288
  192.3 0.1 copy.27
  192.4 15.2 %all_to_all.33 = f32[8,74,128]{2,1,0:T(8,128)S(1)} all-to-all(f32[8,74,128]{2,1,0:T(8,128)S(1)} %copy.27), channel_id=1, replica_groups=mesh['x'=4,'yh'=2,'z'=8,'yl'=2,'c'=2] {'z'}, dimensions={0} | all-to-all | bytes 606208 | tf_op jit(solution)/shard_map/all_to_all | solution.py:280
  207.6 0.6 reshape.39
  208.3 3.2 %all-to-all-start.5 = ((f32[2,12,128]{2,1,0:T(8,128)}), f32[2,12,128]{2,1,0:T(8,128)S(1)}, u32[]{:S(2)}, u32[]{:S(2)}) async-start(f32[2,12,128]{2,1,0:T(8,128)} %reshape.39), calls=%async_computation.5 | async-start | bytes 32768 | tf_op jit(solution)/shard_map/all_to_all | solution.py:280
  211.5 0.1 reshape.41
  211.6 0.6 copy.29
  212.2 0.6 all-to-all-done.5
  212.9 0.6 pad_maximum_fusion.2
  (19 shorter events, 0.2 us)
Async XLA Ops:
  23.5 7.6 %copy-start = (f32[1,2,2,320,320]{4,3,2,1,0:T(8,128)S(1)}, f32[1,2,2,320,320]{4,3,2,1,0:T(8,128)}, u32[]{:S(2)}) copy-start(f32[1,2,2,320,320]{4,3,2,1,0:T(8,128)} %param.7) | copy-start | bytes 4915204
  23.5 27.6 %all-to-all-start.2 = ((f32[16,8,24,128]{3,2,1,0:T(8,128)}), f32[16,8,24,128]{3,2,1,0:T(8,128)S(1)}, u32[]{:S(2)}, u32[]{:S(2)}) async-start(f32[16,8,24,128]{3,2,1,0:T(8,128)} %broadcast_in_dim.18), calls=%async_computation.2 | async-start | bytes 3145728 | tf_op jit(solution)/shard_map/all_to_all | solution.py:280
  32.5 37.1 %collective-permute-start.3 = (f32[2,320,384]{2,1,0:T(8,128)}, f32[2,320,384]{2,1,0:T(8,128)}, u32[]{:S(2)}, u32[]{:S(2)}) collective-permute-start(f32[2,320,384]{2,1,0:T(8,128)} %get-tuple-element.17), channel_id=1, source_target_pairs={{0,34},{2,0},{32,2},{34,32},{1,35},{3,1},{33,3},{35,33},{4,38},{6,... | collective-permute-start | bytes 2949128 | tf_op jit(solution)/shard_map/ppermute | solution.py:292
  35.2 35.6 %copy-start.3 = (s32[2]{0:T(128)S(1)}, s32[2]{0:T(128)}, u32[]{:S(2)}) copy-start(s32[2]{0:T(128)} %param.9) | copy-start | bytes 28
  35.2 35.8 %copy-start.2 = (s32[2,2]{1,0:T(2,128)S(1)}, s32[2,2]{1,0:T(2,128)}, u32[]{:S(2)}) copy-start(s32[2,2]{1,0:T(2,128)} %param.8) | copy-start | bytes 52
  35.2 35.6 %collective-permute-start.2 = (f32[2,320,384]{2,1,0:T(8,128)}, f32[2,320,384]{2,1,0:T(8,128)}, u32[]{:S(2)}, u32[]{:S(2)}) collective-permute-start(f32[2,320,384]{2,1,0:T(8,128)} %get-tuple-element.18), channel_id=1, source_target_pairs={{0,2},{2,32},{32,34},{34,0},{1,3},{3,33},{33,35},{35,1},{4,6},{6,3... | collective-permute-start | bytes 2949128 | tf_op jit(solution)/shard_map/ppermute | solution.py:292
  36.6 37.3 %collective-permute-start.1 = (f32[2,2,320,384]{3,2,1,0:T(8,128)}, f32[2,2,320,384]{3,2,1,0:T(8,128)}, u32[]{:S(2)}, u32[]{:S(2)}) collective-permute-start(f32[2,2,320,384]{3,2,1,0:T(8,128)} %pad.4.own), channel_id=1, source_target_pairs={{0,1},{1,0},{2,3},{3,2},{4,5},{5,4},{6,7},{7,6},{8,9},{9,8},{10,11... | collective-permute-start | bytes 5898248 | tf_op jit(solution)/shard_map/ppermute | solution.py:292
  51.1 22.8 %copy-start.1 = (f32[16,8,24,128]{3,2,1,0:T(8,128)}, f32[16,8,24,128]{3,2,1,0:T(8,128)S(1)}, u32[]{:S(2)}) copy-start(f32[16,8,24,128]{3,2,1,0:T(8,128)S(1)} %all-to-all-done.2) | copy-start | bytes 4718596
  51.1 22.8 %collective-permute-start = (f32[8,2,8,24,128]{4,3,2,1,0:T(8,128)S(1)}, f32[8,2,8,24,128]{4,3,2,1,0:T(8,128)S(1)}, u32[]{:S(2)}, u32[]{:S(2)}) collective-permute-start(f32[8,2,8,24,128]{4,3,2,1,0:T(8,128)S(1)} %bitcast.28), channel_id=1, source_target_pairs={{0,1},{1,0},{2,3},{3,2},{4,5},{5,4},{6,7},{7,6},{8,9},{9,8},{10,11... | collective-permute-start | bytes 4718600 | tf_op jit(solution)/shard_map/ppermute | solution.py:292
  69.6 2.9 %collective-permute-start.5 = (f32[2,320,384]{2,1,0:T(8,128)}, f32[2,320,384]{2,1,0:T(8,128)}, u32[]{:S(2)}, u32[]{:S(2)}) collective-permute-start(f32[2,320,384]{2,1,0:T(8,128)} %collective-permute-done.3.far1), channel_id=1, source_target_pairs={{0,1},{1,0},{2,3},{3,2},{4,5},{5,4},{6,7},{7,6},{8,9},{9,8},{10,11... | collective-permute-start | bytes 2949128 | tf_op jit(solution)/shard_map/ppermute | solution.py:292
  70.8 3.1 %collective-permute-start.4 = (f32[2,320,384]{2,1,0:T(8,128)}, f32[2,320,384]{2,1,0:T(8,128)}, u32[]{:S(2)}, u32[]{:S(2)}) collective-permute-start(f32[2,320,384]{2,1,0:T(8,128)} %collective-permute-done.2.far0), channel_id=1, source_target_pairs={{0,1},{1,0},{2,3},{3,2},{4,5},{5,4},{6,7},{7,6},{8,9},{9,8},{10,11... | collective-permute-start | bytes 2949128 | tf_op jit(solution)/shard_map/ppermute | solution.py:292
  73.9 1.2 copy-start.4
  114.9 8.4 %collective-permute-start.6 = (f32[16,592,128]{2,1,0:T(8,128)}, f32[16,592,128]{2,1,0:T(8,128)S(1)}, u32[]{:S(2)}, u32[]{:S(2)}) collective-permute-start(f32[16,592,128]{2,1,0:T(8,128)} %get-tuple-element.5), channel_id=1, source_target_pairs={{0,1},{1,0},{2,3},{3,2},{4,5},{5,4},{6,7},{7,6},{8,9},{9,8},{10,11... | collective-permute-start | bytes 14549000 | tf_op jit(solution)/shard_map/ppermute | solution.py:292
  208.3 4.6 %all-to-all-start.5 = ((f32[2,12,128]{2,1,0:T(8,128)}), f32[2,12,128]{2,1,0:T(8,128)S(1)}, u32[]{:S(2)}, u32[]{:S(2)}) async-start(f32[2,12,128]{2,1,0:T(8,128)} %reshape.39), calls=%async_computation.5 | async-start | bytes 32768 | tf_op jit(solution)/shard_map/all_to_all | solution.py:280

commit v3 on v2

v3 whole, which is shorter than its diff:
```python
import math

import jax
import jax.numpy as jnp
import numpy as np
from jax import lax
from jax.experimental import pallas as pl
from jax.experimental.pallas import tpu as pltpu
from jax.sharding import Mesh
from jax.sharding import PartitionSpec as P

AXES = ("x", "yh", "z", "yl", "c")
ROWS = 256
CUT = 64
GROUP = 2


def block_matrices(pixels):
    index = np.arange(pixels, dtype=np.int64)
    chirp = ((index[:, None] - index[None, :]) ** 2 % (2 * pixels)) * (math.pi / pixels)
    turn = (index[:, None] * index[None, :] % pixels) * (2.0 * math.pi / pixels)
    scale = 1.0 / math.sqrt(pixels)
    result = []
    for re, im in ((np.cos(chirp), np.sin(chirp)), (np.cos(turn), -np.sin(turn))):
        re, im = (re * scale).astype(jnp.bfloat16), (im * scale).astype(jnp.bfloat16)
        result.append(np.block([[re, im], [-im, re]]))
        result.append(np.block([[re, -im], [im, re]]))
    return np.stack(result)


def dot(a, b):
    return jnp.dot(a, b, preferred_element_type=jnp.float32)


def shift_left(value, lanes, sublanes):
    groups = value.shape[0] // 8
    value = pltpu.roll(value.reshape(groups, 8, 384), lax.rem(8 - sublanes, 8), 1)
    index = lax.broadcasted_iota(jnp.int32, (groups - 1, 8, 384), 1)
    value = jnp.where(index < 8 - sublanes, value[:-1], value[1:]).reshape(8 * groups - 8, 384)
    turn = lax.rem(128 - lanes, 128)
    parts = [pltpu.roll(value[:, a : a + 128], turn, 1) for a in (0, 128, 256)]
    index = lax.broadcasted_iota(jnp.int32, parts[0].shape, 1)
    keep = index < 128 - lanes
    return jnp.concatenate([jnp.where(keep, a, b) for a, b in zip(parts, parts[1:])], axis=1)


def shift_right(value, lanes, sublanes):
    groups = value.shape[0] // 8
    turn = lax.rem(lanes, 128)
    zero = jnp.zeros((value.shape[0], 128), jnp.float32)
    parts = [zero] + [pltpu.roll(value[:, a : a + 128], turn, 1) for a in (0, 128)] + [zero]
    index = lax.broadcasted_iota(jnp.int32, zero.shape, 1)
    moved = index < lanes
    value = jnp.concatenate([jnp.where(moved, a, b) for a, b in zip(parts, parts[1:])], axis=1)
    value = pltpu.roll(value.reshape(groups, 8, 384), lax.rem(sublanes, 8), 1)
    zero = jnp.zeros((1, 8, 384), jnp.float32)
    above, below = jnp.concatenate([zero, value]), jnp.concatenate([value, zero])
    index = lax.broadcasted_iota(jnp.int32, above.shape, 1)
    return jnp.where(index < sublanes, above, below).reshape(8 * groups + 8, 384)


def kernel(
    offsets,
    chosen,
    mine,
    other,
    own,
    partner,
    far0,
    far1,
    cross0,
    cross1,
    amplitudes,
    matrices,
    keep,
    send,
    probe_grad,
    canvas,
    probe,
    tiles,
    packed,
    patch,
    patch_grad,
    wave1,
    wave2,
    tall,
    wide,
    intensity,
    probe_sem,
    tile_sem,
    out_sem,
):
    half = probe_grad.shape[2]
    pixels = 2 * half
    modes = wave1.shape[0]
    positions = tiles.shape[0]
    core, low_y = lax.axis_index("c"), lax.axis_index("yl")
    steps = [slice(i, i + ROWS) for i in range(0, pixels, ROWS)]
    lanes_of = range(GROUP)

    def low(rows):
        return slice(rows.start + pixels, rows.stop + pixels)

    copies = [
        pltpu.make_async_copy(source, packed.at[side], probe_sem.at[i])
        for i, (source, side) in enumerate(((mine, core), (other, 1 - core)))
    ]
    for copy in copies:
        copy.start()
    grad_blocks = packed.reshape(2, 8, 8, 2, 24, half)
    probe_out = [
        pltpu.make_async_copy(
            grad_blocks.at[side, :, z, y],
            target.at[8 * y : 8 * y + 8, 400 + 24 * z : 424 + 24 * z, :],
            out_sem.at[i, y, z],
        )
        for i, (target, side) in enumerate(((keep, core), (send, 1 - core)))
        for y in range(2)
        for z in range(8)
    ]
    canvas_blocks = canvas.reshape(4, 8, 40, 1280)
    canvas_out = [
        pltpu.make_async_copy(
            canvas_blocks.at[2 * i + y, :, :, 128 * j : 128 * j + 128],
            target.at[8 * y : 8 * y + 8, 40 * j : 40 * j + 40, :],
            out_sem.at[i, y, 8 + j],
        )
        for i, target in enumerate((keep, send))
        for y in range(2)
        for j in range(10)
    ]
    for n in range(positions):
        tile = chosen[n]
        kind = 2 * (lax.div(tile, 2) ^ low_y) + (lax.rem(tile, 2) ^ core)
        for source, (first, second) in enumerate(
            ((own.at[0], own.at[1]), (partner.at[0], partner.at[1]), (far0, far1), (cross0, cross1))
        ):

            @pl.when(kind == source)
            def _():
                pltpu.make_async_copy(first, tiles.at[n, 0], tile_sem.at[n, 0]).start()
                pltpu.make_async_copy(second, tiles.at[n, 1], tile_sem.at[n, 1]).start()

    canvas[...] = jnp.zeros_like(canvas)
    probe_grad[...] = jnp.zeros_like(probe_grad)
    for n in range(positions):
        for k in range(2):
            pltpu.make_async_copy(far0, tiles.at[n, k], tile_sem.at[n, k]).wait()
    for copy in copies:
        copy.wait()
    upper = lax.broadcasted_iota(jnp.int32, (8, half), 0) < 4

    def unpack(block, _):
        start = pl.multiple_of(24 * block, 8)
        for side in range(2):
            probe[side, pl.ds(start, 8), :] = packed[0, block, 8 * side : 8 * side + 8, :]
            probe[side, pl.ds(start + 16, 8), :] = packed[1, block, 8 * side : 8 * side + 8, :]
        a, b = packed[0, block, 16:24, :], packed[1, block, 16:24, :]
        probe[0, pl.ds(start + 8, 8), :] = jnp.where(upper, a, b)
        probe[1, pl.ds(start + 8, 8), :] = pltpu.roll(jnp.where(upper, b, a), 4, 0)
        return 0

    def pack(block, _):
        start = pl.multiple_of(24 * block, 8)
        for side in range(2):
            packed[0, block, 8 * side : 8 * side + 8, :] = probe_grad[side, pl.ds(start, 8), :]
            packed[1, block, 8 * side : 8 * side + 8, :] = probe_grad[side, pl.ds(start + 16, 8), :]
        a = probe_grad[0, pl.ds(start + 8, 8), :]
        b = pltpu.roll(probe_grad[1, pl.ds(start + 8, 8), :], 4, 0)
        packed[0, block, 16:24, :] = jnp.where(upper, a, b)
        packed[1, block, 16:24, :] = jnp.where(upper, b, a)
        return 0

    lax.fori_loop(0, packed.shape[1], unpack, 0, unroll=8)

    def window_of(m, part, rows):
        start = pl.multiple_of((part * modes + m) * pixels, pixels) + rows.start
        return pl.ds(pl.multiple_of(start, ROWS), ROWS)

    def load_probe(m, part, rows):
        window = window_of(m, part, rows)
        return jnp.concatenate([probe[0, window, :], probe[1, window, :]], axis=1)

    def position(n, _):
        row, column, tile = offsets[n, 0], offsets[n, 1], chosen[n]
        base = jnp.minimum(lax.div(row, 8) * 8, 56)
        down = row - base
        place = 2 * (lax.rem(tile, 2) ^ core) + lax.div(tile, 2)
        for k in range(2):
            for part in range(2):
                for i in range(0, pixels, CUT):
                    window = pl.ds(pl.multiple_of(base + i, 8), CUT + 8)
                    patch[k, part, i : i + CUT, :] = shift_left(tiles[n, k, part, window, :], column, down)
        patch_grad[...] = jnp.zeros_like(patch_grad)
        intensity[...] = jnp.zeros_like(intensity)

        def forward(group, _):
            first = group * GROUP
            for j in lanes_of:
                for rows in steps:
                    pr, pi = load_probe(first + j, 0, rows), load_probe(first + j, 1, rows)
                    qr, qi = patch[0, 0, rows, :], patch[0, 1, rows, :]
                    tall[j, 0, rows, :] = (pr * qr - pi * qi).astype(jnp.bfloat16)
                    tall[j, 0, low(rows), :] = (pr * qi + pi * qr).astype(jnp.bfloat16)
            for j in lanes_of:
                for rows in steps:
                    a = dot(matrices[1, rows, :], tall[j, 0])
                    wide[j, 0, rows, :pixels] = a.astype(jnp.bfloat16)
                    a = dot(matrices[1, low(rows), :], tall[j, 0])
                    wide[j, 0, rows, pixels:] = a.astype(jnp.bfloat16)
            for j in lanes_of:
                for rows in steps:
                    w = dot(wide[j, 0, rows, :], matrices[0])
                    wave1[first + j, rows, :] = w
                    wr, wi = w[:, :pixels], w[:, pixels:]
                    qr, qi = patch[1, 0, rows, :], patch[1, 1, rows, :]
                    tall[j, 1, rows, :] = (wr * qr - wi * qi).astype(jnp.bfloat16)
                    tall[j, 1, low(rows), :] = (wr * qi + wi * qr).astype(jnp.bfloat16)
            for j in lanes_of:
                for rows in steps:
                    a = dot(matrices[3, rows, :], tall[j, 1])
                    wide[j, 1, rows, :pixels] = a.astype(jnp.bfloat16)
                    a = dot(matrices[3, low(rows), :], tall[j, 1])
                    wide[j, 1, rows, pixels:] = a.astype(jnp.bfloat16)
            for j in lanes_of:
                for rows in steps:
                    w = dot(wide[j, 1, rows, :], matrices[2])
                    wave2[first + j, rows, :] = w
                    wr, wi = w[:, :pixels], w[:, pixels:]
                    intensity[rows, :] += wr * wr + wi * wi
            return 0

        lax.fori_loop(0, modes // GROUP, forward, 0)
        for rows in steps:
            measured = amplitudes[n, rows, :].astype(jnp.float32)
            intensity[rows, :] = 2.0 - 2.0 * measured * lax.rsqrt(intensity[rows, :] + 1.0)

        def backward(group, _):
            first = group * GROUP
            for j in lanes_of:
                for rows in steps:
                    g = intensity[rows, :]
                    w = wave2[first + j, rows, :]
                    d = (w * jnp.concatenate([g, g], axis=1)).astype(jnp.bfloat16)
                    d = dot(d, matrices[3]).astype(jnp.bfloat16)
                    tall[j, 0, rows, :] = d[:, :pixels]
                    tall[j, 0, low(rows), :] = d[:, pixels:]
            for j in lanes_of:
                for rows in steps:
                    dr = dot(matrices[2, rows, :], tall[j, 0])
                    di = dot(matrices[2, low(rows), :], tall[j, 0])
                    wr, wi = wave1[first + j, rows, :pixels], wave1[first + j, rows, pixels:]
                    patch_grad[1, 0, rows, :] += dr * wr + di * wi
                    patch_grad[1, 1, rows, :] += di * wr - dr * wi
                    qr, qi = patch[1, 0, rows, :], patch[1, 1, rows, :]
                    wide[j, 0, rows, :pixels] = (dr * qr + di * qi).astype(jnp.bfloat16)
                    wide[j, 0, rows, pixels:] = (di * qr - dr * qi).astype(jnp.bfloat16)
            for j in lanes_of:
                for rows in steps:
                    d = dot(wide[j, 0, rows, :], matrices[1]).astype(jnp.bfloat16)
                    tall[j, 1, rows, :] = d[:, :pixels]
                    tall[j, 1, low(rows), :] = d[:, pixels:]
            for j in lanes_of:
                for rows in steps:
                    dr = dot(matrices[0, rows, :], tall[j, 1])
                    di = dot(matrices[0, low(rows), :], tall[j, 1])
                    pr, pi = load_probe(first + j, 0, rows), load_probe(first + j, 1, rows)
                    patch_grad[0, 0, rows, :] += dr * pr + di * pi
                    patch_grad[0, 1, rows, :] += di * pr - dr * pi
                    qr, qi = patch[0, 0, rows, :], patch[0, 1, rows, :]
                    for part, value in enumerate((dr * qr + di * qi, di * qr - dr * qi)):
                        window = window_of(first + j, part, rows)
                        probe_grad[0, window, :] += value[:, :half]
                        probe_grad[1, window, :] += value[:, half:]
            return 0

        lax.fori_loop(0, modes // GROUP, backward, 0)

        @pl.when(n == positions - 1)
        def _():
            lax.fori_loop(0, packed.shape[1], pack, 0, unroll=8)
            for copy in probe_out:
                copy.start()

        for k in range(2):
            for part in range(2):
                lane = (k * 2 + part) * 320 - part * 64
                for i in range(0, pixels, CUT):
                    piece = shift_right(patch_grad[k, part, i : i + CUT, :], column + part * 64, down)
                    window = pl.ds(pl.multiple_of(base + i, 8), CUT + 8)
                    canvas[place, window, lane : lane + 384] += piece
        return 0

    lax.fori_loop(0, positions, position, 0)
    for copy in canvas_out:
        copy.start()
    for copy in probe_out + canvas_out:
        copy.wait()


def device_gradients(offsets, chosen, mine, other, tile_parts, amplitudes):
    half = mine.shape[2]
    rows, pixels = mine.shape[0] * mine.shape[1], 2 * half
    modes = rows // (2 * pixels)
    positions = amplitudes.shape[0]
    scalar = pl.BlockSpec(memory_space=pltpu.SMEM)
    whole = pl.BlockSpec(memory_space=pltpu.VMEM)
    there = pl.BlockSpec(memory_space=pl.ANY)
    scratch = [
        pltpu.VMEM((2, rows, half), jnp.float32),
        pltpu.VMEM((4, 320, 1280), jnp.float32),
        pltpu.VMEM((2, rows, half), jnp.float32),
        pltpu.VMEM((positions, 2, 2, 320, 384), jnp.float32),
        pltpu.VMEM((2,) + mine.shape, jnp.float32),
        pltpu.VMEM((2, 2, pixels, pixels), jnp.float32),
        pltpu.VMEM((2, 2, pixels, pixels), jnp.float32),
        pltpu.VMEM((modes, pixels, 2 * pixels), jnp.float32),
        pltpu.VMEM((modes, pixels, 2 * pixels), jnp.float32),
        pltpu.VMEM((GROUP, 2, 2 * pixels, pixels), jnp.bfloat16),
        pltpu.VMEM((GROUP, 2, pixels, 2 * pixels), jnp.bfloat16),
        pltpu.VMEM((pixels, pixels), jnp.float32),
        pltpu.SemaphoreType.DMA((2,)),
        pltpu.SemaphoreType.DMA((positions, 2)),
        pltpu.SemaphoreType.DMA((2, 2, 18)),
    ]
    flops = positions * modes * 8 * 4 * 2 * pixels**3
    return pl.pallas_call(
        kernel,
        out_shape=(jax.ShapeDtypeStruct((16, 592, 128), jnp.float32),) * 2,
        in_specs=[scalar] * 2 + [there] * 8 + [whole] * 2,
        out_specs=(there, there),
        scratch_shapes=scratch,
        cost_estimate=pl.CostEstimate(flops=flops, bytes_accessed=20_000_000, transcendentals=0),
        compiler_params=pltpu.CompilerParams(vmem_limit_bytes=56 * 1024 * 1024),
        name="gradients",
    )(offsets, chosen, mine, other, *tile_parts, amplitudes, jnp.asarray(block_matrices(pixels)))


def exchange(value, axes):
    return lax.all_to_all(value, axes, split_axis=0, concat_axis=0, tiled=True)


def spread(value, axes, count):
    return exchange(jnp.broadcast_to(value[None], (count,) + value.shape), axes)


def reduce_over(value, axes):
    return jnp.sum(exchange(value, axes), axis=0)


def shift(value, axes, count, by):
    return lax.ppermute(value, axes, [(i, (i + by) % count) for i in range(count)])


def device_body(probe_modes, object_tiles, scan_offsets, patch_tiles, amplitudes):
    own_rows, pixels = probe_modes.shape
    half = pixels // 2

    padded = jnp.pad(object_tiles[0], ((0, 0), (0, 0), (0, 0), (0, 64)))
    far0 = shift(padded[0], ("yh", "yl"), 4, 1)
    far1 = shift(padded[1], ("yh", "yl"), 4, 3)
    partner = shift(padded, "c", 2, 1)
    cross0 = shift(far0, "c", 2, 1)
    cross1 = shift(far1, "c", 2, 1)

    first = lax.axis_index("c") == 0
    eight = jnp.where(first, probe_modes[:8], probe_modes[4:])
    four = jnp.where(first, probe_modes[8:], probe_modes[:4])
    mixed = (four[:, :half], four[:, half:])
    mixed = jnp.where(first, jnp.concatenate(mixed), jnp.concatenate(mixed[::-1]))
    piece = jnp.concatenate([eight[:, :half], eight[:, half:], mixed])
    block = spread(piece, ("yh", "z", "yl"), 32)
    mine = spread(block, "x", 4).reshape(128, 2 * own_rows, half)
    other = shift(mine, "c", 2, 1)

    keep, send = device_gradients(
        scan_offsets,
        patch_tiles,
        mine,
        other,
        (padded, partner, far0, far1, cross0, cross1),
        amplitudes,
    )

    total = keep + shift(send, "c", 2, 1)
    total = reduce_over(total, ("yl", "x", "yh"))
    objects = total[:400].reshape(10, 8, 5, 128).transpose(1, 0, 2, 3).reshape(8, 50, 128)
    total = reduce_over(jnp.concatenate([objects, total[400:].reshape(8, 24, 128)], axis=1), "z")
    object_gradient = total[:50].reshape(10, 5, 128).transpose(1, 0, 2).reshape(5, 2, 2, 320)
    object_gradient = object_gradient.transpose(1, 2, 0, 3)[None]
    piece = total[50:]
    eight = jnp.concatenate([piece[:8], piece[8:16]], axis=1)
    four = jnp.where(
        first,
        jnp.concatenate([piece[16:20], piece[20:]], axis=1),
        jnp.concatenate([piece[20:], piece[16:20]], axis=1),
    )
    probe_gradient = jnp.where(first, jnp.concatenate([eight, four]), jnp.concatenate([four, eight]))
    return (probe_gradient, object_gradient)


def solution(mesh):
    fine = Mesh(mesh.devices.reshape(4, 2, 8, 2, 2), AXES)
    scan, tile = AXES[:3], AXES[3:]
    placed = (
        P(AXES, None),
        P(tile, None, None, None, None),
        P(AXES, None),
        P(AXES),
        P(AXES, None, None),
    )
    return jax.shard_map(
        device_body,
        mesh=fine,
        in_specs=placed,
        out_specs=(P(AXES, None), P(tile, None, None, scan, None)),
        check_vma=False,
    )
```

time: 217 us -> 188 us (0.87); the launches traced: 213 us -> 187 us
  waiting for transfers between devices: 45.1 us -> 30.3 us
  Pallas kernels: 39.8 us -> 27.4 us
  blocking collectives: 99.4 us -> 106 us
  starting transfers between devices: 13.6 us -> 7.1 us
    pallas_call x1, Pallas kernels: 39.8 us -> 27.4 us  [device_gradients(): pl.pallas_call(kernel, out_shape=(jax.ShapeDtypeStruct((16, 592, 128), jn...]
    ppermute x7, waiting for transfers between devices: 30 us -> 18.4 us  [shift(): lax.ppermute(value, axes, [(i, (i + by) % count) for i in range(count)])]
    all_to_all x4 -> x3, blocking collectives: 99.4 us -> 106 us  [exchange(): return lax.all_to_all(value, axes, split_axis=0, concat_axis=0, tiled=True)]
    all_to_all x2 -> x1, starting transfers between devices: 10.8 us -> 4.9 us  [exchange(): return lax.all_to_all(value, axes, split_axis=0, concat_axis=0, tiled=True)]
    all_to_all x2 -> x1, waiting for transfers between devices: 15.1 us -> 11.9 us  [exchange(): return lax.all_to_all(value, axes, split_axis=0, concat_axis=0, tiled=True)]
  transfers between devices with their start and end apart: 9 -> 8, of which waited for: 7 -> 6; matrix products, arithmetic and copies ran while one was open for 2% -> 2% of each run, Pallas kernels for 0% -> 0%
where the time goes in v3:
time: 188 us; the launch traced here: 187 us
  blocking collectives  106 us (56%)
  waiting for transfers between devices  30.3 us (16%)
  Pallas kernels  27.4 us (15%)
  local copies, waits for them, and re-layouts  7.84 us (4%)
  other arithmetic  7.68 us (4%)
  starting transfers between devices  7.1 us (4%)
    all_to_all x3, blocking collectives, exchange(): return lax.all_to_all(value, axes, split_axis=0, concat_axis=0, tiled=True)  106 us
    pallas_call x1, Pallas kernels, device_gradients(): pl.pallas_call(kernel, out_shape=(jax.ShapeDtypeStruct((16, 592, 128), jn...  27.4 us
    ppermute x7, waiting for transfers between devices, shift(): lax.ppermute(value, axes, [(i, (i + by) % count) for i in range(count)])  18.4 us
    all_to_all x1, waiting for transfers between devices, exchange(): return lax.all_to_all(value, axes, split_axis=0, concat_axis=0, tiled=True)  11.9 us
    all_to_all x1, starting transfers between devices, exchange(): return lax.all_to_all(value, axes, split_axis=0, concat_axis=0, tiled=True)  4.9 us
  transfers between devices with their start and end apart: 8, of which 6 were waited for; matrix products, arithmetic and copies ran while one was open for 2% of the time, Pallas kernels for 0%

profile of v3, /device:TPU:6, one launch (start us, length us, event | category | flops | bytes accessed | tf_op | source)
XLA Modules:
  0.0 186.7 jit_solution(5206913489751557581)
XLA Ops:
  0.6 0.7 slice_select_fusion.1
  1.4 0.8 slice_select_fusion
  2.2 27.8 %all_to_all.20 = f32[32,24,128]{2,1,0:T(8,128)S(1)} all-to-all(f32[32,24,128]{2,1,0:T(8,128)S(1)} %broadcast_in_dim.6), channel_id=1, replica_groups=mesh['x'=4,'yh'=2,'z'=8,'yl'=2,'c'=2] {'yh','z','yl'}, dimensions={0} | all-to-all | bytes 786432 | tf_op jit(solution)/shard_map/all_to_all | solution.py:340
  30.0 1.3 broadcast_in_dim.7
  31.3 0.0 copy-start
  31.3 4.9 %all-to-all-start.1 = ((f32[4,32,24,128]{3,2,1,0:T(8,128)}), f32[4,32,24,128]{3,2,1,0:T(8,128)S(1)}, u32[]{:S(2)}, u32[]{:S(2)}) async-start(f32[4,32,24,128]{3,2,1,0:T(8,128)} %broadcast_in_dim.7), calls=%async_computation.1 | async-start | bytes 3145728 | tf_op jit(solution)/shard_map/all_to_all | solution.py:340
  36.2 0.0 copy-done
  36.2 1.4 slice_bitcast_fusion
  37.6 0.5 collective-permute-start.3
  38.1 1.5 collective-permute-start.2
  39.6 1.4 pad.4.own
  41.0 0.0 collective-permute-start.1
  41.0 11.9 %all-to-all-done.1 = f32[4,32,24,128]{3,2,1,0:T(8,128)S(1)} async-done(((f32[4,32,24,128]{3,2,1,0:T(8,128)}), f32[4,32,24,128]{3,2,1,0:T(8,128)S(1)}, u32[]{:S(2)}, u32[]{:S(2)}) %all-to-all-start.1) | async-done | bytes 1572896 | tf_op jit(solution)/shard_map/all_to_all | solution.py:340
  53.0 0.0 copy-start.1
  53.0 0.0 collective-permute-start
  53.0 6.0 %collective-permute-done.3.far1 = f32[2,320,384]{2,1,0:T(8,128)} collective-permute-done((f32[2,320,384]{2,1,0:T(8,128)}, f32[2,320,384]{2,1,0:T(8,128)}, u32[]{:S(2)}, u32[]{:S(2)}) %collective-permute-start.3) | collective-permute-done | bytes 983072 | tf_op jit(solution)/shard_map/ppermute | solution.py:352
  59.0 0.0 collective-permute-start.5
  59.0 1.2 collective-permute-done.2.far0
  60.2 0.0 collective-permute-start.4
  60.2 1.6 collective-permute-done.5.cross1
  61.8 0.0 copy-start.4
  61.8 1.4 collective-permute-done.4.cross0
  63.2 0.0 copy-start.5
  63.2 0.0 collective-permute-done.1.partner
  63.2 0.0 copy-start.2
  63.2 0.0 collective-permute-done.other
  63.2 0.0 copy-done.1
  63.2 0.0 copy-done.4
  63.2 0.9 copy-done.5
  64.1 0.7 copy-done.2
  64.9 0.0 copy-start.3
  64.9 1.1 copy-done.3
  66.0 27.4 %gradients.1 = (f32[16,592,128]{2,1,0:T(8,128)}, f32[16,592,128]{2,1,0:T(8,128)}) custom-call(s32[2,2]{1,0:T(2,128)} %offsets.1, s32[2]{0:T(128)} %chosen.1, f32[128,24,128]{2,1,0:T(8,128)} %bitcast.18, f32[128,24,128]{2,1,0:T(8,128)} %copy-done.3, f32[2,2,320,384]{3,2,1,0:T(8,128)} %pad.4.own, f32[2,2,320,384]{3,2,1,0:T(8,128)} %copy-done.2, ...), custom_call_target="tpu_custom_call" | custom-call | flops 12884901888 | bytes 20000000 | tf_op jit(solution)/shard_map/gradients/pallas_call | solution.py:327
  93.4 0.2 collective-permute-start.6
  93.5 8.2 %collective-permute-done.6 = f32[16,592,128]{2,1,0:T(8,128)S(1)} collective-permute-done((f32[16,592,128]{2,1,0:T(8,128)}, f32[16,592,128]{2,1,0:T(8,128)S(1)}, u32[]{:S(2)}, u32[]{:S(2)}) %collective-permute-start.6) | collective-permute-done | bytes 4849696 | tf_op jit(solution)/shard_map/ppermute | solution.py:352
  101.8 2.9 %add.5 = f32[16,592,128]{2,1,0:T(8,128)S(1)} add(f32[16,592,128]{2,1,0:T(8,128)} %get-tuple-element.4, f32[16,592,128]{2,1,0:T(8,128)S(1)} %collective-permute-done.6) | non-fusion elementwise | flops 1212416 | bytes 14548992 | tf_op jit(solution)/shard_map/add | solution.py:385
  104.6 61.9 %all_to_all.21 = f32[16,592,128]{2,1,0:T(8,128)} all-to-all(f32[16,592,128]{2,1,0:T(8,128)S(1)} %add.5), channel_id=1, replica_groups=mesh['x'=4,'yh'=2,'z'=8,'yl'=2,'c'=2] {'yl','x','yh'}, dimensions={0} | all-to-all | bytes 9699328 | tf_op jit(solution)/shard_map/all_to_all | solution.py:340
  166.5 2.6 %reduce_sum.18 = f32[592,128]{1,0:T(8,128)S(1)} reduce(f32[16,592,128]{2,1,0:T(8,128)} %all_to_all.21, f32[]{:T(128)} %constant.10.clone.1), dimensions={0}, to_apply=%region_0.1 | reduce | flops 1136640 | bytes 5152772 | tf_op jit(solution)/shard_map/reduce_sum | solution.py:348
  169.4 0.1 copy.17
  169.4 15.8 %all_to_all.22 = f32[8,74,128]{2,1,0:T(8,128)S(1)} all-to-all(f32[8,74,128]{2,1,0:T(8,128)S(1)} %copy.17), channel_id=1, replica_groups=mesh['x'=4,'yh'=2,'z'=8,'yl'=2,'c'=2] {'z'}, dimensions={0} | all-to-all | bytes 606208 | tf_op jit(solution)/shard_map/all_to_all | solution.py:340
  185.3 0.1 reshape.29
  185.4 0.6 copy.19
  186.1 0.6 maximum_select_fusion
  (17 shorter events, 0.2 us)
Async XLA Ops:
  31.3 4.9 %copy-start = (f32[1,2,2,320,320]{4,3,2,1,0:T(8,128)S(1)}, f32[1,2,2,320,320]{4,3,2,1,0:T(8,128)}, u32[]{:S(2)}) copy-start(f32[1,2,2,320,320]{4,3,2,1,0:T(8,128)} %param.7) | copy-start | bytes 4915204
  31.3 21.7 %all-to-all-start.1 = ((f32[4,32,24,128]{3,2,1,0:T(8,128)}), f32[4,32,24,128]{3,2,1,0:T(8,128)S(1)}, u32[]{:S(2)}, u32[]{:S(2)}) async-start(f32[4,32,24,128]{3,2,1,0:T(8,128)} %broadcast_in_dim.7), calls=%async_computation.1 | async-start | bytes 3145728 | tf_op jit(solution)/shard_map/all_to_all | solution.py:340
  37.6 21.4 %collective-permute-start.3 = (f32[2,320,384]{2,1,0:T(8,128)}, f32[2,320,384]{2,1,0:T(8,128)}, u32[]{:S(2)}, u32[]{:S(2)}) collective-permute-start(f32[2,320,384]{2,1,0:T(8,128)} %get-tuple-element.12), channel_id=1, source_target_pairs={{0,34},{2,0},{32,2},{34,32},{1,35},{3,1},{33,3},{35,33},{4,38},{6,... | collective-permute-start | bytes 2949128 | tf_op jit(solution)/shard_map/ppermute | solution.py:352
  38.1 22.1 %collective-permute-start.2 = (f32[2,320,384]{2,1,0:T(8,128)}, f32[2,320,384]{2,1,0:T(8,128)}, u32[]{:S(2)}, u32[]{:S(2)}) collective-permute-start(f32[2,320,384]{2,1,0:T(8,128)} %get-tuple-element.13), channel_id=1, source_target_pairs={{0,2},{2,32},{32,34},{34,0},{1,3},{3,33},{33,35},{35,1},{4,6},{6,3... | collective-permute-start | bytes 2949128 | tf_op jit(solution)/shard_map/ppermute | solution.py:352
  41.0 22.1 %collective-permute-start.1 = (f32[2,2,320,384]{3,2,1,0:T(8,128)}, f32[2,2,320,384]{3,2,1,0:T(8,128)S(1)}, u32[]{:S(2)}, u32[]{:S(2)}) collective-permute-start(f32[2,2,320,384]{3,2,1,0:T(8,128)} %pad.4.own), channel_id=1, source_target_pairs={{0,1},{1,0},{2,3},{3,2},{4,5},{5,4},{6,7},{7,6},{8,9},{9,8},{10,11... | collective-permute-start | bytes 5898248 | tf_op jit(solution)/shard_map/ppermute | solution.py:352
  53.0 10.2 %copy-start.1 = (f32[4,32,24,128]{3,2,1,0:T(8,128)}, f32[4,32,24,128]{3,2,1,0:T(8,128)S(1)}, u32[]{:S(2)}) copy-start(f32[4,32,24,128]{3,2,1,0:T(8,128)S(1)} %all-to-all-done.1) | copy-start | bytes 4718596
  53.0 10.2 %collective-permute-start = (f32[128,24,128]{2,1,0:T(8,128)S(1)}, f32[128,24,128]{2,1,0:T(8,128)S(1)}, u32[]{:S(2)}, u32[]{:S(2)}) collective-permute-start(f32[128,24,128]{2,1,0:T(8,128)S(1)} %bitcast.17), channel_id=1, source_target_pairs={{0,1},{1,0},{2,3},{3,2},{4,5},{5,4},{6,7},{7,6},{8,9},{9,8},{10,11... | collective-permute-start | bytes 4718600 | tf_op jit(solution)/shard_map/ppermute | solution.py:352
  59.0 2.8 %collective-permute-start.5 = (f32[2,320,384]{2,1,0:T(8,128)}, f32[2,320,384]{2,1,0:T(8,128)S(1)}, u32[]{:S(2)}, u32[]{:S(2)}) collective-permute-start(f32[2,320,384]{2,1,0:T(8,128)} %collective-permute-done.3.far1), channel_id=1, source_target_pairs={{0,1},{1,0},{2,3},{3,2},{4,5},{5,4},{6,7},{7,6},{8,9},{9,8},{10,11... | collective-permute-start | bytes 2949128 | tf_op jit(solution)/shard_map/ppermute | solution.py:352
  60.2 3.0 %collective-permute-start.4 = (f32[2,320,384]{2,1,0:T(8,128)}, f32[2,320,384]{2,1,0:T(8,128)S(1)}, u32[]{:S(2)}, u32[]{:S(2)}) collective-permute-start(f32[2,320,384]{2,1,0:T(8,128)} %collective-permute-done.2.far0), channel_id=1, source_target_pairs={{0,1},{1,0},{2,3},{3,2},{4,5},{5,4},{6,7},{7,6},{8,9},{9,8},{10,11... | collective-permute-start | bytes 2949128 | tf_op jit(solution)/shard_map/ppermute | solution.py:352
  61.8 1.4 copy-start.4
  63.2 1.0 copy-start.5
  63.2 1.7 copy-start.2
  64.9 1.1 copy-start.3
  93.4 8.4 %collective-permute-start.6 = (f32[16,592,128]{2,1,0:T(8,128)}, f32[16,592,128]{2,1,0:T(8,128)S(1)}, u32[]{:S(2)}, u32[]{:S(2)}) collective-permute-start(f32[16,592,128]{2,1,0:T(8,128)} %get-tuple-element.5), channel_id=1, source_target_pairs={{0,1},{1,0},{2,3},{3,2},{4,5},{5,4},{6,7},{7,6},{8,9},{9,8},{10,11... | collective-permute-start | bytes 14549000 | tf_op jit(solution)/shard_map/ppermute | solution.py:352

commit v4 on v3

--- a/solution.py
+++ b/solution.py
@@ -101,9 +101,11 @@
     def low(rows):
         return slice(rows.start + pixels, rows.stop + pixels)
 
+    blocks = packed.reshape(2, 8, 8, 2, 24, half)
     copies = [
-        pltpu.make_async_copy(source, packed.at[side], probe_sem.at[i])
+        pltpu.make_async_copy(source.at[:, y], blocks.at[side, :, :, y], probe_sem.at[i, y])
         for i, (source, side) in enumerate(((mine, core), (other, 1 - core)))
+        for y in range(2)
     ]
     for copy in copies:
         copy.start()
@@ -190,7 +192,8 @@
             for part in range(2):
                 for i in range(0, pixels, CUT):
                     window = pl.ds(pl.multiple_of(base + i, 8), CUT + 8)
-                    patch[k, part, i : i + CUT, :] = shift_left(tiles[n, k, part, window, :], column, down)
+                    piece = tiles[n, k, window, 256 * part : 256 * part + 384]
+                    patch[k, part, i : i + CUT, :] = shift_left(piece, column + 64 * part, down)
         patch_grad[...] = jnp.zeros_like(patch_grad)
         intensity[...] = jnp.zeros_like(intensity)
 
@@ -299,8 +302,8 @@
 
 
 def device_gradients(offsets, chosen, mine, other, tile_parts, amplitudes):
-    half = mine.shape[2]
-    rows, pixels = mine.shape[0] * mine.shape[1], 2 * half
+    half = mine.shape[-1]
+    rows, pixels = math.prod(mine.shape[:-1]), 2 * half
     modes = rows // (2 * pixels)
     positions = amplitudes.shape[0]
     scalar = pl.BlockSpec(memory_space=pltpu.SMEM)
@@ -310,8 +313,8 @@
         pltpu.VMEM((2, rows, half), jnp.float32),
         pltpu.VMEM((4, 320, 1280), jnp.float32),
         pltpu.VMEM((2, rows, half), jnp.float32),
-        pltpu.VMEM((positions, 2, 2, 320, 384), jnp.float32),
-        pltpu.VMEM((2,) + mine.shape, jnp.float32),
+        pltpu.VMEM((positions, 2, 320, 640), jnp.float32),
+        pltpu.VMEM((2, rows // 24, 24, half), jnp.float32),
         pltpu.VMEM((2, 2, pixels, pixels), jnp.float32),
         pltpu.VMEM((2, 2, pixels, pixels), jnp.float32),
         pltpu.VMEM((modes, pixels, 2 * pixels), jnp.float32),
@@ -319,7 +322,7 @@
         pltpu.VMEM((GROUP, 2, 2 * pixels, pixels), jnp.bfloat16),
         pltpu.VMEM((GROUP, 2, pixels, 2 * pixels), jnp.bfloat16),
         pltpu.VMEM((pixels, pixels), jnp.float32),
-        pltpu.SemaphoreType.DMA((2,)),
+        pltpu.SemaphoreType.DMA((2, 2)),
         pltpu.SemaphoreType.DMA((positions, 2)),
         pltpu.SemaphoreType.DMA((2, 2, 18)),
     ]
@@ -331,7 +334,7 @@
         out_specs=(there, there),
         scratch_shapes=scratch,
         cost_estimate=pl.CostEstimate(flops=flops, bytes_accessed=20_000_000, transcendentals=0),
-        compiler_params=pltpu.CompilerParams(vmem_limit_bytes=56 * 1024 * 1024),
+        compiler_params=pltpu.CompilerParams(vmem_limit_bytes=40 * 1024 * 1024),
         name="gradients",
     )(offsets, chosen, mine, other, *tile_parts, amplitudes, jnp.asarray(block_matrices(pixels)))
 
@@ -356,12 +359,15 @@
     own_rows, pixels = probe_modes.shape
     half = pixels // 2
 
-    padded = jnp.pad(object_tiles[0], ((0, 0), (0, 0), (0, 0), (0, 64)))
-    far0 = shift(padded[0], ("yh", "yl"), 4, 1)
-    far1 = shift(padded[1], ("yh", "yl"), 4, 3)
-    partner = shift(padded, "c", 2, 1)
-    cross0 = shift(far0, "c", 2, 1)
-    cross1 = shift(far1, "c", 2, 1)
+    joined = jnp.concatenate([object_tiles[0, :, 0], object_tiles[0, :, 1]], axis=2)
+    far0 = shift(joined[0], ("yh", "yl"), 4, 1)
+    far1 = shift(joined[1], ("yh", "yl"), 4, 3)
+    partner = shift(joined, "c", 2, 1)
+    zero = probe_modes[0, 0] * 0.0
+    relay0 = far0 + zero
+    relay1 = far1 + zero
+    cross0 = shift(relay0, "c", 2, 1)
+    cross1 = shift(relay1, "c", 2, 1)
 
     first = lax.axis_index("c") == 0
     eight = jnp.where(first, probe_modes[:8], probe_modes[4:])
@@ -369,8 +375,8 @@
     mixed = (four[:, :half], four[:, half:])
     mixed = jnp.where(first, jnp.concatenate(mixed), jnp.concatenate(mixed[::-1]))
     piece = jnp.concatenate([eight[:, :half], eight[:, half:], mixed])
-    block = spread(piece, ("yh", "z", "yl"), 32)
-    mine = spread(block, "x", 4).reshape(128, 2 * own_rows, half)
+    block = spread(piece, "z", 8)
+    mine = spread(block, ("x", "yh", "yl"), 16).reshape(8, 2, 8, 2 * own_rows, half)
     other = shift(mine, "c", 2, 1)
 
     keep, send = device_gradients(
@@ -378,7 +384,7 @@
         patch_tiles,
         mine,
         other,
-        (padded, partner, far0, far1, cross0, cross1),
+        (joined, partner, far0, far1, cross0, cross1),
         amplitudes,
     )
 

time: 188 us -> 189 us (level)
  blocking collectives: 106 us -> 95.5 us
  waiting for transfers between devices: 30.3 us -> 38.3 us
  other arithmetic: 7.68 us -> 12 us
  starting transfers between devices: 7.1 us -> 11.4 us
  local copies, waits for them, and re-layouts: 7.84 us -> 3.59 us
  Pallas kernels: 27.4 us -> 25.2 us
    all_to_all x3, blocking collectives: 106 us -> 95.5 us  [exchange(): return lax.all_to_all(value, axes, split_axis=0, concat_axis=0, tiled=True)]
    ppermute x7, waiting for transfers between devices: 18.4 us -> 23.1 us  [shift(): lax.ppermute(value, axes, [(i, (i + by) % count) for i in range(count)])]
    all_to_all x1, waiting for transfers between devices: 11.9 us -> 15.2 us  [exchange(): return lax.all_to_all(value, axes, split_axis=0, concat_axis=0, tiled=True)]
    unnamed x13 -> x11, local copies, waits for them, and re-layouts: 3.43 us -> 0.64 us
    all_to_all x1, starting transfers between devices: 4.9 us -> 7.56 us  [exchange(): return lax.all_to_all(value, axes, split_axis=0, concat_axis=0, tiled=True)]
    add x0 -> x2, other arithmetic: none -> 2.56 us  [the longest x1 1.35 us: device_body(): relay1 = far1 + zero]
    pallas_call x1, Pallas kernels: 27.4 us -> 25.2 us  [device_gradients(): pl.pallas_call(kernel, out_shape=(jax.ShapeDtypeStruct((16, 592, 128), jn...]
  transfers between devices with their start and end apart: 8 -> 8, of which waited for: 6 -> 5; matrix products, arithmetic and copies ran while one was open for 2% -> 3% of each run, Pallas kernels for 0% -> 0%
where the time goes in v4:
time: 189 us; the launch traced here: 188 us
  blocking collectives  95.5 us (51%)
  waiting for transfers between devices  38.3 us (20%)
  Pallas kernels  25.2 us (13%)
  other arithmetic  12 us (6%)
  starting transfers between devices  11.4 us (6%)
  local copies, waits for them, and re-layouts  3.59 us (2%)
    all_to_all x3, blocking collectives, exchange(): return lax.all_to_all(value, axes, split_axis=0, concat_axis=0, tiled=True)  95.5 us
    pallas_call x1, Pallas kernels, device_gradients(): pl.pallas_call(kernel, out_shape=(jax.ShapeDtypeStruct((16, 592, 128), jn...  25.2 us
    ppermute x7, waiting for transfers between devices, shift(): lax.ppermute(value, axes, [(i, (i + by) % count) for i in range(count)])  23.1 us
    all_to_all x1, waiting for transfers between devices, exchange(): return lax.all_to_all(value, axes, split_axis=0, concat_axis=0, tiled=True)  15.2 us
    all_to_all x1, starting transfers between devices, exchange(): return lax.all_to_all(value, axes, split_axis=0, concat_axis=0, tiled=True)  7.56 us
    ppermute x7, starting transfers between devices, shift(): lax.ppermute(value, axes, [(i, (i + by) % count) for i in range(count)])  3.89 us
  transfers between devices with their start and end apart: 8, of which 5 were waited for; matrix products, arithmetic and copies ran while one was open for 3% of the time, Pallas kernels for 0%

profile of v4, /device:TPU:6, one launch (start us, length us, event | category | flops | bytes accessed | tf_op | source)
XLA Modules:
  0.0 187.6 jit_solution(16858794283298595430)
XLA Ops:
  0.6 0.7 slice_select_fusion.1
  1.4 0.8 slice_select_fusion
  2.2 17.0 %all_to_all.20 = f32[8,24,128]{2,1,0:T(8,128)S(1)} all-to-all(f32[8,24,128]{2,1,0:T(8,128)S(1)} %broadcast_in_dim.6), channel_id=1, replica_groups=mesh['x'=4,'yh'=2,'z'=8,'yl'=2,'c'=2] {'z'}, dimensions={0} | all-to-all | bytes 196608 | tf_op jit(solution)/shard_map/all_to_all | solution.py:343
  19.2 1.3 broadcast_in_dim.7
  20.5 0.0 copy-start.4
  20.5 7.6 %all-to-all-start.1 = ((f32[16,8,24,128]{3,2,1,0:T(8,128)}), f32[16,8,24,128]{3,2,1,0:T(8,128)S(1)}, u32[]{:S(2)}, u32[]{:S(2)}) async-start(f32[16,8,24,128]{3,2,1,0:T(8,128)} %broadcast_in_dim.7), calls=%async_computation.1 | async-start | bytes 3145728 | tf_op jit(solution)/shard_map/all_to_all | solution.py:343
  28.1 0.0 copy-done.4
  28.1 0.1 slice_bitcast_fusion.1
  28.2 1.5 fusion.3
  29.7 2.7 %collective-permute-start.3 = (f32[320,640]{1,0:T(8,128)}, f32[320,640]{1,0:T(8,128)}, u32[]{:S(2)}, u32[]{:S(2)}) collective-permute-start(f32[320,640]{1,0:T(8,128)} %get-tuple-element.12), channel_id=1, source_target_pairs={{0,34},{2,0},{32,2},{34,32},{1,35},{3,1},{33,3},{35,33},{4,38},{6,... | collective-permute-start | bytes 2457608 | tf_op jit(solution)/shard_map/ppermute | solution.py:355
  32.4 0.0 collective-permute-start.2
  32.4 0.3 pad_maximum_fusion.own
  32.7 0.1 collective-permute-start.1
  32.8 15.2 %all-to-all-done.1 = f32[16,8,24,128]{3,2,1,0:T(8,128)S(1)} async-done(((f32[16,8,24,128]{3,2,1,0:T(8,128)}), f32[16,8,24,128]{3,2,1,0:T(8,128)S(1)}, u32[]{:S(2)}, u32[]{:S(2)}) %all-to-all-start.1) | async-done | bytes 1572896 | tf_op jit(solution)/shard_map/all_to_all | solution.py:343
  48.0 0.0 collective-permute-start
  48.0 1.2 slice.79
  49.9 13.1 %collective-permute-done.3.far1 = f32[320,640]{1,0:T(8,128)} collective-permute-done((f32[320,640]{1,0:T(8,128)}, f32[320,640]{1,0:T(8,128)}, u32[]{:S(2)}, u32[]{:S(2)}) %collective-permute-start.3) | collective-permute-done | bytes 819232 | tf_op jit(solution)/shard_map/ppermute | solution.py:355
  63.0 0.0 copy-start
  63.0 0.0 copy-start.1
  63.0 0.0 copy-start.2
  63.0 0.0 copy-start.3
  63.0 1.4 broadcast_add_fusion
  64.4 0.1 collective-permute-start.5
  64.5 0.0 collective-permute-done.2.far0
  64.5 1.2 broadcast_add_fusion.1
  65.7 0.6 collective-permute-start.4
  66.3 0.5 collective-permute-done.5.cross1
  66.8 1.4 collective-permute-done.4.cross0
  68.2 0.0 collective-permute-done.1.partner
  68.2 0.0 collective-permute-done.other
  68.2 0.0 copy-done
  68.3 0.0 copy-done.1
  68.3 0.0 copy-done.2
  68.3 0.0 copy-done.3
  68.3 25.2 %gradients.1 = (f32[16,592,128]{2,1,0:T(8,128)}, f32[16,592,128]{2,1,0:T(8,128)}) custom-call(s32[2,2]{1,0:T(2,128)S(1)} %copy-done.1, s32[2]{0:T(128)S(1)} %copy-done.2, f32[8,2,8,24,128]{4,3,2,1,0:T(8,128)S(1)} %bitcast.24, f32[8,2,8,24,128]{4,3,2,1,0:T(8,128)S(1)} %collective-permute-done.other, f32[2,320,640]{2,1,0:T(8,128)S(1)} %pad_maximum_fusion.own, ...), custom_call_target="tpu_custom_call" | custom-call | flops 12884901888 | bytes 20000000 | tf_op jit(solution)/shard_map/gradients/pallas_call | solution.py:330
  93.5 0.5 collective-permute-start.6
  94.0 7.9 %collective-permute-done.6 = f32[16,592,128]{2,1,0:T(8,128)S(1)} collective-permute-done((f32[16,592,128]{2,1,0:T(8,128)}, f32[16,592,128]{2,1,0:T(8,128)S(1)}, u32[]{:S(2)}, u32[]{:S(2)}) %collective-permute-start.6) | collective-permute-done | bytes 4849696 | tf_op jit(solution)/shard_map/ppermute | solution.py:355
  101.9 2.9 %add.16 = f32[16,592,128]{2,1,0:T(8,128)S(1)} add(f32[16,592,128]{2,1,0:T(8,128)} %get-tuple-element.4, f32[16,592,128]{2,1,0:T(8,128)S(1)} %collective-permute-done.6) | non-fusion elementwise | flops 1212416 | bytes 14548992 | tf_op jit(solution)/shard_map/add | solution.py:391
  104.8 63.2 %all_to_all.21 = f32[16,592,128]{2,1,0:T(8,128)} all-to-all(f32[16,592,128]{2,1,0:T(8,128)S(1)} %add.16), channel_id=1, replica_groups=mesh['x'=4,'yh'=2,'z'=8,'yl'=2,'c'=2] {'yl','x','yh'}, dimensions={0} | all-to-all | bytes 9699328 | tf_op jit(solution)/shard_map/all_to_all | solution.py:343
  168.0 2.6 %reduce_sum.18 = f32[592,128]{1,0:T(8,128)S(1)} reduce(f32[16,592,128]{2,1,0:T(8,128)} %all_to_all.21, f32[]{:T(128)} %constant.11.clone.1), dimensions={0}, to_apply=%region_0.1 | reduce | flops 1136640 | bytes 5152772 | tf_op jit(solution)/shard_map/reduce_sum | solution.py:351
  170.8 0.1 copy.25
  170.9 15.3 %all_to_all.22 = f32[8,74,128]{2,1,0:T(8,128)S(1)} all-to-all(f32[8,74,128]{2,1,0:T(8,128)S(1)} %copy.25), channel_id=1, replica_groups=mesh['x'=4,'yh'=2,'z'=8,'yl'=2,'c'=2] {'z'}, dimensions={0} | all-to-all | bytes 606208 | tf_op jit(solution)/shard_map/all_to_all | solution.py:343
  186.2 0.1 reshape.31
  186.3 0.6 copy.27
  186.9 0.6 maximum_select_fusion
  (17 shorter events, 0.2 us)
Async XLA Ops:
  20.5 7.6 %copy-start.4 = (f32[1,2,2,320,320]{4,3,2,1,0:T(8,128)S(1)}, f32[1,2,2,320,320]{4,3,2,1,0:T(8,128)}, u32[]{:S(2)}) copy-start(f32[1,2,2,320,320]{4,3,2,1,0:T(8,128)} %param.7) | copy-start | bytes 4915204
  20.5 27.5 %all-to-all-start.1 = ((f32[16,8,24,128]{3,2,1,0:T(8,128)}), f32[16,8,24,128]{3,2,1,0:T(8,128)S(1)}, u32[]{:S(2)}, u32[]{:S(2)}) async-start(f32[16,8,24,128]{3,2,1,0:T(8,128)} %broadcast_in_dim.7), calls=%async_computation.1 | async-start | bytes 3145728 | tf_op jit(solution)/shard_map/all_to_all | solution.py:343
  29.7 33.3 %collective-permute-start.3 = (f32[320,640]{1,0:T(8,128)}, f32[320,640]{1,0:T(8,128)}, u32[]{:S(2)}, u32[]{:S(2)}) collective-permute-start(f32[320,640]{1,0:T(8,128)} %get-tuple-element.12), channel_id=1, source_target_pairs={{0,34},{2,0},{32,2},{34,32},{1,35},{3,1},{33,3},{35,33},{4,38},{6,... | collective-permute-start | bytes 2457608 | tf_op jit(solution)/shard_map/ppermute | solution.py:355
  32.4 32.1 %collective-permute-start.2 = (f32[320,640]{1,0:T(8,128)}, f32[320,640]{1,0:T(8,128)}, u32[]{:S(2)}, u32[]{:S(2)}) collective-permute-start(f32[320,640]{1,0:T(8,128)} %get-tuple-element.13), channel_id=1, source_target_pairs={{0,2},{2,32},{32,34},{34,0},{1,3},{3,33},{33,35},{35,1},{4,6},{6,3... | collective-permute-start | bytes 2457608 | tf_op jit(solution)/shard_map/ppermute | solution.py:355
  32.7 35.6 %collective-permute-start.1 = (f32[2,320,640]{2,1,0:T(8,128)S(1)}, f32[2,320,640]{2,1,0:T(8,128)}, u32[]{:S(2)}, u32[]{:S(2)}) collective-permute-start(f32[2,320,640]{2,1,0:T(8,128)S(1)} %pad_maximum_fusion.own), channel_id=1, source_target_pairs={{0,1},{1,0},{2,3},{3,2},{4,5},{5,4},{6,7},{7,6},{8,9},{9,8},{10,11... | collective-permute-start | bytes 4915208 | tf_op jit(solution)/shard_map/ppermute | solution.py:355
  48.0 20.2 %collective-permute-start = (f32[8,2,8,24,128]{4,3,2,1,0:T(8,128)S(1)}, f32[8,2,8,24,128]{4,3,2,1,0:T(8,128)S(1)}, u32[]{:S(2)}, u32[]{:S(2)}) collective-permute-start(f32[8,2,8,24,128]{4,3,2,1,0:T(8,128)S(1)} %bitcast.23), channel_id=1, source_target_pairs={{0,1},{1,0},{2,3},{3,2},{4,5},{5,4},{6,7},{7,6},{8,9},{9,8},{10,11... | collective-permute-start | bytes 4718600 | tf_op jit(solution)/shard_map/ppermute | solution.py:355
  63.0 5.2 %copy-start = (bf16[2,256,256]{2,1,0:T(8,128)(2,1)S(1)}, bf16[2,256,256]{2,1,0:T(8,128)(2,1)}, u32[]{:S(2)}) copy-start(bf16[2,256,256]{2,1,0:T(8,128)(2,1)} %amplitudes.1) | copy-start | bytes 786436
  63.0 5.2 %copy-start.1 = (s32[2,2]{1,0:T(2,128)S(1)}, s32[2,2]{1,0:T(2,128)}, u32[]{:S(2)}) copy-start(s32[2,2]{1,0:T(2,128)} %offsets.1) | copy-start | bytes 52
  63.0 5.2 %copy-start.2 = (s32[2]{0:T(128)S(1)}, s32[2]{0:T(128)}, u32[]{:S(2)}) copy-start(s32[2]{0:T(128)} %chosen.1) | copy-start | bytes 28
  63.0 5.2 %copy-start.3 = (bf16[4,512,512]{2,1,0:T(8,128)(2,1)S(1)}, bf16[4,512,512]{2,1,0:T(8,128)(2,1)}, u32[]{:S(2)}) copy-start(bf16[4,512,512]{2,1,0:T(8,128)(2,1)} %constant.12.clone.matrices) | copy-start | bytes 6291460
  64.4 2.4 %collective-permute-start.5 = (f32[320,640]{1,0:T(8,128)S(1)}, f32[320,640]{1,0:T(8,128)S(1)}, u32[]{:S(2)}, u32[]{:S(2)}) collective-permute-start(f32[320,640]{1,0:T(8,128)S(1)} %broadcast_add_fusion), channel_id=1, source_target_pairs={{0,1},{1,0},{2,3},{3,2},{4,5},{5,4},{6,7},{7,6},{8,9},{9,8},{10,11... | collective-permute-start | bytes 2457608 | tf_op jit(solution)/shard_map/ppermute | solution.py:355
  65.7 2.5 %collective-permute-start.4 = (f32[320,640]{1,0:T(8,128)S(1)}, f32[320,640]{1,0:T(8,128)S(1)}, u32[]{:S(2)}, u32[]{:S(2)}) collective-permute-start(f32[320,640]{1,0:T(8,128)S(1)} %broadcast_add_fusion.1), channel_id=1, source_target_pairs={{0,1},{1,0},{2,3},{3,2},{4,5},{5,4},{6,7},{7,6},{8,9},{9,8},{10,11... | collective-permute-start | bytes 2457608 | tf_op jit(solution)/shard_map/ppermute | solution.py:355
  93.5 8.4 %collective-permute-start.6 = (f32[16,592,128]{2,1,0:T(8,128)}, f32[16,592,128]{2,1,0:T(8,128)S(1)}, u32[]{:S(2)}, u32[]{:S(2)}) collective-permute-start(f32[16,592,128]{2,1,0:T(8,128)} %get-tuple-element.5), channel_id=1, source_target_pairs={{0,1},{1,0},{2,3},{3,2},{4,5},{5,4},{6,7},{7,6},{8,9},{9,8},{10,11... | collective-permute-start | bytes 14549000 | tf_op jit(solution)/shard_map/ppermute | solution.py:355
